TPU v7x, 256 devices: a whole 4x4x8 slice. The times are simulated.
256 devices in a mesh: gx: 8 (over y, z_hi), gy: 8 (over z_lo, core), gz: 4 (over x).
Axes of the slice: x: 4, y: 4, z: 8 (z_hi: 2, z_lo: 4; z = z_hi * 4 + z_lo), core: 2. Of those that a mesh axis runs over, the one named last changes fastest.
Arguments:
- right_side: float32 [3, 64, 64, 512], P(None, 'gx', 'gy', 'gz'), may hold values from -17 to 17
- phase_labels: int32 [32, 32, 256], P('gx', 'gy', 'gz'), may hold values from 0 to 7
- phase_moduli: float32 [8], replicated, may hold values from 0.03 to 0.3
- coarse_nodes: int32 [64, 64, 512], P('gx', 'gy', 'gz'), may hold values from 0 to 5
- coarse_inverse: float32 [9216, 9216], P(('gx', 'gy', 'gz')), as said below
Outputs:
- solution_field: float32 [3, 64, 64, 512], P(None, 'gx', 'gy', 'gz')
- residual: float32 [3, 64, 64, 512], P(None, 'gx', 'gy', 'gz')
Inputs may be any that keep to these rules, and one draw needn't show every extreme that they name: `coarse_inverse`: symmetric.
All inputs are finite; a program needn't handle non-finite values.
Results may differ from a plain program's by a relative error of at most 0.0003.
Values sent between devices are 32-bit elements; how exact they have to be, the bound alone decides.
A program may use at most 64 MiB of HBM per device.

v0:
```python
import jax
import jax.numpy as jnp
from jax import lax
from jax.sharding import PartitionSpec as P

SWEEPS = 4
ITERS = 2


bond_ratio = 0.5
relax = 0.6
highest = lax.Precision.HIGHEST
neighbour_offsets = tuple(
    (
        (shift_x, shift_y, shift_z)
        for shift_x in (-1, 0, 1)
        for shift_y in (-1, 0, 1)
        for shift_z in (-1, 0, 1)
        if shift_x * shift_x + shift_y * shift_y + shift_z * shift_z > 0
    )
)


def extended(x, sides, width):
    for axis, dim in sides:
        size, length = (lax.axis_size(axis), x.shape[dim])
        up = [(i, (i + 1) % size) for i in range(size - 1)]
        down = [(j, i) for i, j in up]
        last = lax.slice_in_dim(x, length - width, length, axis=dim)
        leading = lax.slice_in_dim(x, 0, width, axis=dim)
        before = lax.ppermute(last, axis, up)
        after = lax.ppermute(leading, axis, down)
        x = jnp.concatenate([before, x, after], axis=dim)
    return x


def inner_view(array, shift_x, shift_y, shift_z):
    size_x, size_y, size_z = array.shape[-3:]
    return array[
        ...,
        1 + shift_x : size_x - 1 + shift_x,
        1 + shift_y : size_y - 1 + shift_y,
        1 + shift_z : size_z - 1 + shift_z,
    ]


def spring_force(field_pad, stiff_pad):
    centre = inner_view(field_pad, 0, 0, 0)
    stiff_centre = inner_view(stiff_pad, 0, 0, 0)
    parts = [jnp.zeros_like(centre[0]) for component in range(3)]
    for offset in neighbour_offsets:
        length = offset[0] * offset[0] + offset[1] * offset[1] + offset[2] * offset[2]
        spring = (
            0.5 * (stiff_centre + inner_view(stiff_pad, offset[0], offset[1], offset[2])) / length
        )
        partner = inner_view(field_pad, offset[0], offset[1], offset[2])
        stretch = [centre[component] - partner[component] for component in range(3)]
        projected = jnp.zeros_like(stretch[0])
        for component in range(3):
            if offset[component] != 0:
                projected = projected + offset[component] * stretch[component]
        for component in range(3):
            summand = stretch[component]
            if offset[component] != 0:
                summand = summand + bond_ratio * offset[component] / length * projected
            parts[component] = parts[component] + spring * summand
    return jnp.stack(parts)


def diagonal(stiff_pad):
    stiff_centre = inner_view(stiff_pad, 0, 0, 0)
    parts = [jnp.zeros_like(stiff_centre) for component in range(3)]
    for offset in neighbour_offsets:
        length = offset[0] * offset[0] + offset[1] * offset[1] + offset[2] * offset[2]
        spring = (
            0.5 * (stiff_centre + inner_view(stiff_pad, offset[0], offset[1], offset[2])) / length
        )
        for component in range(3):
            parts[component] = parts[component] + spring * (
                1.0 + bond_ratio * offset[component] * offset[component] / length
            )
    return jnp.stack(parts)


def local_solve(residual_ext, stiff_rim, diag_ext):
    widths = [(0, 0)] * (residual_ext.ndim - 3) + [(1, 1)] * 3
    solution = relax * residual_ext / diag_ext
    for sweep in range(SWEEPS - 1):
        solution = (
            solution
            + relax * (residual_ext - spring_force(jnp.pad(solution, widths), stiff_rim)) / diag_ext
        )
    return solution


def cross(first, second):
    return jnp.stack(
        [
            first[1] * second[2] - first[2] * second[1],
            first[2] * second[0] - first[0] * second[2],
            first[0] * second[1] - first[1] * second[0],
        ]
    )


def local_coords(size_x, size_y, size_z):
    along_x = ((2.0 * jnp.arange(size_x, dtype=jnp.float32) + 1.0) / size_x - 1.0).reshape(
        size_x, 1, 1
    )
    along_y = ((2.0 * jnp.arange(size_y, dtype=jnp.float32) + 1.0) / size_y - 1.0).reshape(
        1, size_y, 1
    )
    along_z = ((2.0 * jnp.arange(size_z, dtype=jnp.float32) + 1.0) / size_z - 1.0).reshape(
        1, 1, size_z
    )
    return (along_x, along_y, along_z)


def fold_axis(spread, axis):
    size = spread.shape[axis]
    count = size - 4
    inner = lax.slice_in_dim(spread, 2, size - 2, axis=axis)
    lower = lax.slice_in_dim(spread, 0, 1, axis=axis)
    upper = lax.slice_in_dim(spread, size - 1, size, axis=axis)
    head = lax.slice_in_dim(inner, 0, 1, axis=axis) + lower
    tail = lax.slice_in_dim(inner, count - 1, count, axis=axis) + upper
    middle = lax.slice_in_dim(inner, 1, count - 1, axis=axis)
    return jnp.concatenate([head, middle, tail], axis=axis)


def body(right_side, phase_labels, phase_moduli, coarse_nodes, coarse_inverse):
    phases = phase_moduli.shape[0]
    matches = phase_labels[None] == jnp.arange(phases, dtype=jnp.int32)[:, None, None, None]
    coarse_stiff = jnp.sum(jnp.where(matches, phase_moduli[:, None, None, None], 0.0), axis=0)
    stiffness = jnp.repeat(jnp.repeat(jnp.repeat(coarse_stiff, 2, axis=0), 2, axis=1), 2, axis=2)
    stiff_rim = extended(stiffness, (("gx", 0), ("gy", 1), ("gz", 2)), 2)
    diag_ext = diagonal(stiff_rim)
    stiff_near = stiff_rim[1:-1, 1:-1, 1:-1]
    size_x, size_y, size_z = stiffness.shape
    coords = local_coords(size_x, size_y, size_z)
    node_count = coarse_inverse.shape[0] // 6
    onehot = (
        jnp.arange(node_count, dtype=jnp.int32)[:, None] == coarse_nodes.reshape(1, -1)
    ).astype(jnp.float32)

    def accumulate(piece):
        return jnp.dot(coarse_inverse, piece, precision=highest)

    def coarse_part(residual):
        moments = jnp.concatenate([residual, cross(coords, residual)], axis=0).reshape(6, -1)
        node_sums = jnp.einsum("gc,mc->gm", onehot, moments, precision=highest).reshape(-1)
        solved = accumulate(lax.all_gather(node_sums, ("gx", "gy", "gz"), axis=0, tiled=True))
        per_cell = jnp.einsum("gm,gc->mc", solved.reshape(node_count, 6), onehot, precision=highest)
        per_cell = per_cell.reshape(6, size_x, size_y, size_z)
        return per_cell[:3] + cross(per_cell[3:], coords)

    def local_part(residual_ext):
        solution = local_solve(residual_ext, stiff_rim, diag_ext)
        spread = extended(solution, (("gx", 1), ("gy", 2), ("gz", 3)), 1)
        return fold_axis(fold_axis(fold_axis(spread, 1), 2), 3)

    def widen(vector):
        return extended(vector, (("gx", 1), ("gy", 2), ("gz", 3)), 1)

    def precondition(residual_form):
        return local_part(widen(residual_form)) + coarse_part(residual_form)

    residual = right_side
    solution_field = jnp.zeros_like(right_side)

    def global_sum(value):
        return lax.psum(value, ("gx", "gy", "gz"))

    search = precondition(residual)
    norm_now = global_sum(jnp.sum(residual * search))
    direction = search
    for step in range(ITERS):
        image = spring_force(widen(direction), stiff_near)
        step_size = norm_now / global_sum(jnp.sum(direction * image))
        solution_field = solution_field + step_size * direction
        residual = residual - step_size * image
        if step + 1 < ITERS:
            search = precondition(residual)
            norm_next = global_sum(jnp.sum(residual * search))
            direction = search + norm_next / norm_now * direction
            norm_now = norm_next
    return (solution_field, residual)


def solution(mesh):
    in_specs = (
        P(None, "gx", "gy", "gz"),
        P("gx", "gy", "gz"),
        P(),
        P("gx", "gy", "gz"),
        P(("gx", "gy", "gz"), None),
    )
    out_specs = (P(None, "gx", "gy", "gz"), P(None, "gx", "gy", "gz"))
    return jax.shard_map(body, mesh=mesh, in_specs=in_specs, out_specs=out_specs, check_vma=False)
```

profile of v0, /device:TPU:1, one launch (start us, length us, event | category | flops | bytes accessed | tf_op | source)
XLA Modules:
  0.0 682.7 jit_solution(17536681381676741998)
XLA Ops:
  1.8 9.8 %collective-permute-start.6 = (f32[2,8,128]{2,1,0:T(8,128)S(1)}, f32[2,8,128]{2,1,0:T(8,128)S(1)}, u32[]{:S(2)}, u32[]{:S(2)}) collective-permute-start(f32[2,8,128]{2,1,0:T(8,128)S(1)} %broadcast_in_dim.51), channel_id=1, source_target_pairs={{0,32},{32,64},{64,96},{96,128},{128,160},{160,192},{192,224},{1,3... | collective-permute-start | bytes 24584 | tf_op jit(solution)/shard_map/ppermute | solution.py:31
  13.8 7.9 %collective-permute-start = (f32[3,1,8,128]{3,2,1,0:T(8,128)S(1)}, f32[3,1,8,128]{3,2,1,0:T(8,128)S(1)}, u32[]{:S(2)}, u32[]{:S(2)}) collective-permute-start(f32[3,1,8,128]{3,2,1,0:T(8,128)S(1)} %get-tuple-element.274), channel_id=1, source_target_pairs={{0,32},{32,64},{64,96},{96,128},{128,160},{160,192},{192,224},{1,3... | collective-permute-start | bytes 36872 | tf_op jit(solution)/shard_map/ppermute | solution.py:31
  26.5 79.8 %all-reduce.6 = f32[9216]{0:T(1024)S(1)} all-reduce(f32[9216]{0:T(1024)S(1)} %dynamic-update-slice), channel_id=1, replica_groups=mesh['gx'=8,'gy'=8,'gz'=4] {'gx','gy','gz'}, use_global_device_ids=true, to_apply=%add.6 | all-reduce | flops 9216 | bytes 73728
  109.1 3.2 collective-permute-start.8
  114.3 3.0 collective-permute-done.9
  117.5 2.2 collective-permute-start.10
  121.0 2.2 collective-permute-start.2
  123.2 2.1 collective-permute-start.3
  128.4 4.3 collective-permute-start.4
  136.1 4.1 collective-permute-done.5
  144.8 2.6 fusion.1589
  152.9 2.3 fusion.1585
  159.1 5.2 collective-permute-start.12
  166.0 7.6 %collective-permute-done.13 = f32[3,1,10,130]{3,2,1,0:T(8,128)S(1)} collective-permute-done((f32[3,1,10,130]{3,2,1,0:T(8,128)S(1)}, f32[3,1,10,130]{3,2,1,0:T(8,128)S(1)}, u32[]{:S(2)}, u32[]{:S(2)}) %collective-permute-start.13) | collective-permute-done | bytes 15632 | tf_op jit(solution)/shard_map/ppermute | solution.py:32
  173.7 4.0 collective-permute-start.14
  179.7 3.3 collective-permute-done.15
  183.3 2.5 collective-permute-start.16
  187.2 3.7 collective-permute-done.16
  190.9 4.1 collective-permute-done.17
  197.7 5.2 collective-permute-start.18
  204.2 7.5 %collective-permute-done.19 = f32[3,1,8,128]{3,2,1,0:T(8,128)S(1)} collective-permute-done((f32[3,1,8,128]{3,2,1,0:T(8,128)S(1)}, f32[3,1,8,128]{3,2,1,0:T(8,128)S(1)}, u32[]{:S(2)}, u32[]{:S(2)}) %collective-permute-start.19) | collective-permute-done | bytes 12320 | tf_op jit(solution)/shard_map/ppermute | solution.py:32
  211.7 5.1 collective-permute-start.20
  219.0 3.0 collective-permute-done.21
  222.2 2.8 collective-permute-start.22
  226.5 6.0 collective-permute-done.23
  240.8 74.1 %all-reduce.8 = (f32[]{:T(128)}, f32[]{:T(128)}) all-reduce(f32[]{:T(128)} %get-tuple-element.29, f32[]{:T(128)} %fusion.1595), channel_id=1, replica_groups=mesh['gx'=8,'gy'=8,'gz'=4] {'gx','gy','gz'}, use_global_device_ids=true, to_apply=%region_2.3 | all-reduce | flops 2 | bytes 16 | tf_op jit(solution)/shard_map/psum | solution.py:172
  319.5 4.6 collective-permute-start.24
  330.7 77.3 %all-reduce.7 = f32[9216]{0:T(1024)} all-reduce(f32[9216]{0:T(1024)} %dynamic-update-slice.1), channel_id=1, replica_groups=mesh['gx'=8,'gy'=8,'gz'=4] {'gx','gy','gz'}, use_global_device_ids=true, to_apply=%add.7 | all-reduce | flops 9216 | bytes 73728
  410.2 4.2 collective-permute-start.26
  414.4 2.6 convolution_bitcast_fusion
  424.1 2.3 collective-permute-start.28
  429.7 4.1 collective-permute-done.29
  445.0 2.1 fusion.1576
  450.9 3.9 collective-permute-start.30
  457.0 7.2 %collective-permute-done.31 = f32[3,1,10,130]{3,2,1,0:T(8,128)S(1)} collective-permute-done((f32[3,1,10,130]{3,2,1,0:T(8,128)S(1)}, f32[3,1,10,130]{3,2,1,0:T(8,128)S(1)}, u32[]{:S(2)}, u32[]{:S(2)}) %collective-permute-start.31) | collective-permute-done | bytes 15632 | tf_op jit(solution)/shard_map/ppermute | solution.py:32
  464.2 4.6 collective-permute-start.32
  470.8 3.3 collective-permute-done.33
  474.4 2.5 collective-permute-start.34
  478.3 3.7 collective-permute-done.34
  482.0 4.1 collective-permute-done.35
  488.8 75.1 %psum.30 = f32[]{:T(128)} all-reduce(f32[]{:T(128)} %get-tuple-element.18), channel_id=1, replica_groups=mesh['gx'=8,'gy'=8,'gz'=4] {'gx','gy','gz'}, use_global_device_ids=true, to_apply=%region_6.7 | all-reduce | flops 1 | bytes 8 | tf_op jit(solution)/shard_map/psum | solution.py:172
  565.2 5.2 collective-permute-start.36
  571.7 7.0 %collective-permute-done.37 = f32[3,1,8,128]{3,2,1,0:T(8,128)S(1)} collective-permute-done((f32[3,1,8,128]{3,2,1,0:T(8,128)S(1)}, f32[3,1,8,128]{3,2,1,0:T(8,128)S(1)}, u32[]{:S(2)}, u32[]{:S(2)}) %collective-permute-start.37) | collective-permute-done | bytes 12320 | tf_op jit(solution)/shard_map/ppermute | solution.py:32
  578.8 3.7 collective-permute-start.38
  584.5 3.0 collective-permute-done.39
  587.7 2.4 collective-permute-start.40
  591.7 6.0 collective-permute-done.41
  606.7 73.8 %psum.31 = f32[]{:T(128)} all-reduce(f32[]{:T(128)} %fusion.1594), channel_id=1, replica_groups=mesh['gx'=8,'gy'=8,'gz'=4] {'gx','gy','gz'}, use_global_device_ids=true, to_apply=%region_8.9 | all-reduce | flops 1 | bytes 8 | tf_op jit(solution)/shard_map/psum | solution.py:172
  (483 shorter events, 114.7 us)
Async XLA Ops:
  0.6 105.7 %copy-start = (f32[36,9216]{1,0:T(8,128)S(1)}, f32[36,9216]{1,0:T(8,128)}, u32[]{:S(2)}) copy-start(f32[36,9216]{1,0:T(8,128)} %param.9) | copy-start | bytes 3981316
  1.8 105.9 %copy-start.120 = (s32[8,8,128]{2,1,0:T(8,128)S(1)}, s32[8,8,128]{2,1,0:T(8,128)}, u32[]{:S(2)}) copy-start(s32[8,8,128]{2,1,0:T(8,128)} %param.8) | copy-start | bytes 98308
  1.8 107.3 %collective-permute-start.6 = (f32[2,8,128]{2,1,0:T(8,128)S(1)}, f32[2,8,128]{2,1,0:T(8,128)S(1)}, u32[]{:S(2)}, u32[]{:S(2)}) collective-permute-start(f32[2,8,128]{2,1,0:T(8,128)S(1)} %broadcast_in_dim.51), channel_id=1, source_target_pairs={{0,32},{32,64},{64,96},{96,128},{128,160},{160,192},{192,224},{1,3... | collective-permute-start | bytes 24584 | tf_op jit(solution)/shard_map/ppermute | solution.py:31
  11.7 97.4 %collective-permute-start.7 = (f32[2,8,128]{2,1,0:T(8,128)S(1)}, f32[2,8,128]{2,1,0:T(8,128)S(1)}, u32[]{:S(2)}, u32[]{:S(2)}) collective-permute-start(f32[2,8,128]{2,1,0:T(8,128)S(1)} %broadcast_in_dim.59), channel_id=1, source_target_pairs={{32,0},{64,32},{96,64},{128,96},{160,128},{192,160},{224,192},{33,... | collective-permute-start | bytes 24584 | tf_op jit(solution)/shard_map/ppermute | solution.py:32
  13.8 100.5 %collective-permute-start = (f32[3,1,8,128]{3,2,1,0:T(8,128)S(1)}, f32[3,1,8,128]{3,2,1,0:T(8,128)S(1)}, u32[]{:S(2)}, u32[]{:S(2)}) collective-permute-start(f32[3,1,8,128]{3,2,1,0:T(8,128)S(1)} %get-tuple-element.274), channel_id=1, source_target_pairs={{0,32},{32,64},{64,96},{96,128},{128,160},{160,192},{192,224},{1,3... | collective-permute-start | bytes 36872 | tf_op jit(solution)/shard_map/ppermute | solution.py:31
  21.6 92.7 %collective-permute-start.1 = (f32[3,1,8,128]{3,2,1,0:T(8,128)S(1)}, f32[3,1,8,128]{3,2,1,0:T(8,128)S(1)}, u32[]{:S(2)}, u32[]{:S(2)}) collective-permute-start(f32[3,1,8,128]{3,2,1,0:T(8,128)S(1)} %get-tuple-element.273), channel_id=1, source_target_pairs={{32,0},{64,32},{96,64},{128,96},{160,128},{192,160},{224,192},{33,... | collective-permute-start | bytes 36872 | tf_op jit(solution)/shard_map/ppermute | solution.py:32
  23.0 85.7 %copy-start.124 = (f32[8]{0:T(128)}, f32[8]{0:T(128)S(1)}, u32[]{:S(2)}) copy-start(f32[8]{0:T(128)S(1)} %multiply_add_fusion.115) | copy-start | bytes 100
  23.0 85.7 %copy-start.127 = (f32[128]{0:T(128)}, f32[128]{0:T(128)S(1)}, u32[]{:S(2)}) copy-start(f32[128]{0:T(128)S(1)} %multiply_add_fusion.114) | copy-start | bytes 1540
  109.1 5.2 collective-permute-start.8
  112.3 5.0 collective-permute-start.9
  117.5 7.8 %collective-permute-start.10 = (f32[12,12,2]{2,1,0:T(8,128)S(1)}, f32[12,12,2]{2,1,0:T(8,128)S(1)}, u32[]{:S(2)}, u32[]{:S(2)}) collective-permute-start(f32[12,12,2]{2,1,0:T(8,128)S(1)} %get-tuple-element.271), channel_id=1, source_target_pairs={{0,1},{1,2},{2,3},{4,5},{5,6},{6,7},{8,9},{9,10},{10,11},{12,13},{... | collective-permute-start | bytes 3464 | tf_op jit(solution)/shard_map/ppermute | solution.py:31
  119.6 5.7 collective-permute-start.11
  121.0 6.1 collective-permute-start.2
  123.2 5.0 collective-permute-start.3
  128.4 7.7 %collective-permute-start.4 = (f32[3,10,10,1]{3,0,2,1:T(4,128)S(1)}, f32[3,10,10,1]{3,0,2,1:T(4,128)S(1)}, u32[]{:S(2)}, u32[]{:S(2)}) collective-permute-start(f32[3,10,10,1]{3,0,2,1:T(4,128)S(1)} %get-tuple-element.241), channel_id=1, source_target_pairs={{0,1},{1,2},{2,3},{4,5},{5,6},{6,7},{8,9},{9,10},{10,11},{12,13},{... | collective-permute-start | bytes 3608 | tf_op jit(solution)/shard_map/ppermute | solution.py:31
  132.7 7.5 %collective-permute-start.5 = (f32[3,10,10,1]{3,0,2,1:T(4,128)S(1)}, f32[3,10,10,1]{3,0,2,1:T(4,128)S(1)}, u32[]{:S(2)}, u32[]{:S(2)}) collective-permute-start(f32[3,10,10,1]{3,0,2,1:T(4,128)S(1)} %get-tuple-element.242), channel_id=1, source_target_pairs={{1,0},{2,1},{3,2},{5,4},{6,5},{7,6},{9,8},{10,9},{11,10},{13,12},{... | collective-permute-start | bytes 3608 | tf_op jit(solution)/shard_map/ppermute | solution.py:32
  159.1 6.9 %collective-permute-start.12 = (f32[3,1,10,130]{3,2,1,0:T(8,128)S(1)}, f32[3,1,10,130]{3,2,1,0:T(8,128)S(1)}, u32[]{:S(2)}, u32[]{:S(2)}) collective-permute-start(f32[3,1,10,130]{3,2,1,0:T(8,128)S(1)} %get-tuple-element.107), channel_id=1, source_target_pairs={{0,32},{32,64},{64,96},{96,128},{128,160},{160,192},{192,224},{1,3... | collective-permute-start | bytes 46808 | tf_op jit(solution)/shard_map/ppermute | solution.py:31
  164.3 9.3 %collective-permute-start.13 = (f32[3,1,10,130]{3,2,1,0:T(8,128)S(1)}, f32[3,1,10,130]{3,2,1,0:T(8,128)S(1)}, u32[]{:S(2)}, u32[]{:S(2)}) collective-permute-start(f32[3,1,10,130]{3,2,1,0:T(8,128)S(1)} %get-tuple-element.108), channel_id=1, source_target_pairs={{32,0},{64,32},{96,64},{128,96},{160,128},{192,160},{224,192},{33,... | collective-permute-start | bytes 46808 | tf_op jit(solution)/shard_map/ppermute | solution.py:32
  166.0 74.0 %copy-start.110 = (f32[1,8192]{1,0:T(1,128)}, f32[1,8192]{1,0:T(1,128)S(1)}, u32[]{:S(2)}) copy-start(f32[1,8192]{1,0:T(1,128)S(1)} %get-tuple-element.226) | copy-start | bytes 98308
  166.0 74.0 %copy-start.112 = (f32[1,8192]{1,0:T(1,128)}, f32[1,8192]{1,0:T(1,128)S(1)}, u32[]{:S(2)}) copy-start(f32[1,8192]{1,0:T(1,128)S(1)} %get-tuple-element.227) | copy-start | bytes 98308
  173.7 5.9 collective-permute-start.14
  177.7 5.3 collective-permute-start.15
  183.3 7.6 %collective-permute-start.16 = (f32[3,12,12,1]{3,2,1,0:T(8,128)S(1)}, f32[3,12,12,1]{3,2,1,0:T(8,128)S(1)}, u32[]{:S(2)}, u32[]{:S(2)}) collective-permute-start(f32[3,12,12,1]{3,2,1,0:T(8,128)S(1)} %get-tuple-element.101), channel_id=1, source_target_pairs={{0,1},{1,2},{2,3},{4,5},{5,6},{6,7},{8,9},{9,10},{10,11},{12,13},{... | collective-permute-start | bytes 5192 | tf_op jit(solution)/shard_map/ppermute | solution.py:31
  185.8 9.2 %collective-permute-start.17 = (f32[3,12,12,1]{3,2,1,0:T(8,128)S(1)}, f32[3,12,12,1]{3,2,1,0:T(8,128)S(1)}, u32[]{:S(2)}, u32[]{:S(2)}) collective-permute-start(f32[3,12,12,1]{3,2,1,0:T(8,128)S(1)} %get-tuple-element.102), channel_id=1, source_target_pairs={{1,0},{2,1},{3,2},{5,4},{6,5},{7,6},{9,8},{10,9},{11,10},{13,12},{... | collective-permute-start | bytes 5192 | tf_op jit(solution)/shard_map/ppermute | solution.py:32
  197.7 6.5 collective-permute-start.18
  202.9 8.8 %collective-permute-start.19 = (f32[3,1,8,128]{3,2,1,0:T(8,128)S(1)}, f32[3,1,8,128]{3,2,1,0:T(8,128)S(1)}, u32[]{:S(2)}, u32[]{:S(2)}) collective-permute-start(f32[3,1,8,128]{3,2,1,0:T(8,128)S(1)} %get-tuple-element.270), channel_id=1, source_target_pairs={{32,0},{64,32},{96,64},{128,96},{160,128},{192,160},{224,192},{33,... | collective-permute-start | bytes 36872 | tf_op jit(solution)/shard_map/ppermute | solution.py:32
  211.7 7.1 %collective-permute-start.20 = (f32[3,10,1,128]{3,2,1,0:T(1,128)S(1)}, f32[3,10,1,128]{3,2,1,0:T(1,128)S(1)}, u32[]{:S(2)}, u32[]{:S(2)}) collective-permute-start(f32[3,10,1,128]{3,2,1,0:T(1,128)S(1)} %get-tuple-element.255), channel_id=1, source_target_pairs={{0,4},{4,8},{8,12},{12,16},{16,20},{20,24},{24,28},{1,5},{5,9},{9,... | collective-permute-start | bytes 46088 | tf_op jit(solution)/shard_map/ppermute | solution.py:31
  216.9 5.0 collective-permute-start.21
  222.2 12.9 %collective-permute-start.22 = (f32[3,10,10,1]{3,0,2,1:T(4,128)S(1)}, f32[3,10,10,1]{3,0,2,1:T(4,128)S(1)}, u32[]{:S(2)}, u32[]{:S(2)}) collective-permute-start(f32[3,10,10,1]{3,0,2,1:T(4,128)S(1)} %get-tuple-element.239), channel_id=1, source_target_pairs={{0,1},{1,2},{2,3},{4,5},{5,6},{6,7},{8,9},{9,10},{10,11},{12,13},{... | collective-permute-start | bytes 3608 | tf_op jit(solution)/shard_map/ppermute | solution.py:31
  225.0 7.5 %collective-permute-start.23 = (f32[3,10,10,1]{3,0,2,1:T(4,128)S(1)}, f32[3,10,10,1]{3,0,2,1:T(4,128)S(1)}, u32[]{:S(2)}, u32[]{:S(2)}) collective-permute-start(f32[3,10,10,1]{3,0,2,1:T(4,128)S(1)} %get-tuple-element.240), channel_id=1, source_target_pairs={{1,0},{2,1},{3,2},{5,4},{6,5},{7,6},{9,8},{10,9},{11,10},{13,12},{... | collective-permute-start | bytes 3608 | tf_op jit(solution)/shard_map/ppermute | solution.py:32
  319.5 88.4 %collective-permute-start.24 = (f32[3,1,8,128]{3,2,1,0:T(8,128)}, f32[3,1,8,128]{3,2,1,0:T(8,128)}, u32[]{:S(2)}, u32[]{:S(2)}) collective-permute-start(f32[3,1,8,128]{3,2,1,0:T(8,128)} %get-tuple-element.267), channel_id=1, source_target_pairs={{0,32},{32,64},{64,96},{96,128},{128,160},{160,192},{192,224},{1,3... | collective-permute-start | bytes 36872 | tf_op jit(solution)/shard_map/ppermute | solution.py:31
  324.2 83.8 %collective-permute-start.25 = (f32[3,1,8,128]{3,2,1,0:T(8,128)}, f32[3,1,8,128]{3,2,1,0:T(8,128)}, u32[]{:S(2)}, u32[]{:S(2)}) collective-permute-start(f32[3,1,8,128]{3,2,1,0:T(8,128)} %get-tuple-element.268), channel_id=1, source_target_pairs={{32,0},{64,32},{96,64},{128,96},{160,128},{192,160},{224,192},{33,... | collective-permute-start | bytes 36872 | tf_op jit(solution)/shard_map/ppermute | solution.py:32
  410.2 10.2 %collective-permute-start.26 = (f32[3,10,1,128]{3,2,1,0:T(1,128)}, f32[3,10,1,128]{3,2,1,0:T(1,128)}, u32[]{:S(2)}, u32[]{:S(2)}) collective-permute-start(f32[3,10,1,128]{3,2,1,0:T(1,128)} %get-tuple-element.252), channel_id=1, source_target_pairs={{0,4},{4,8},{8,12},{12,16},{16,20},{20,24},{24,28},{1,5},{5,9},{9,... | collective-permute-start | bytes 46088 | tf_op jit(solution)/shard_map/ppermute | solution.py:31
  418.4 5.4 collective-permute-start.27
  424.1 5.7 collective-permute-start.28
  426.4 7.5 %collective-permute-start.29 = (f32[3,10,10,1]{3,0,2,1:T(4,128)S(1)}, f32[3,10,10,1]{3,0,2,1:T(4,128)S(1)}, u32[]{:S(2)}, u32[]{:S(2)}) collective-permute-start(f32[3,10,10,1]{3,0,2,1:T(4,128)S(1)} %get-tuple-element.238), channel_id=1, source_target_pairs={{1,0},{2,1},{3,2},{5,4},{6,5},{7,6},{9,8},{10,9},{11,10},{13,12},{... | collective-permute-start | bytes 3608 | tf_op jit(solution)/shard_map/ppermute | solution.py:32
  450.9 6.1 collective-permute-start.30
  454.8 9.4 %collective-permute-start.31 = (f32[3,1,10,130]{3,2,1,0:T(8,128)S(1)}, f32[3,1,10,130]{3,2,1,0:T(8,128)S(1)}, u32[]{:S(2)}, u32[]{:S(2)}) collective-permute-start(f32[3,1,10,130]{3,2,1,0:T(8,128)S(1)} %get-tuple-element.106), channel_id=1, source_target_pairs={{32,0},{64,32},{96,64},{128,96},{160,128},{192,160},{224,192},{33,... | collective-permute-start | bytes 46808 | tf_op jit(solution)/shard_map/ppermute | solution.py:32
  464.2 6.5 collective-permute-start.32
  468.8 5.3 collective-permute-start.33
  474.4 7.6 %collective-permute-start.34 = (f32[3,12,12,1]{3,2,1,0:T(8,128)S(1)}, f32[3,12,12,1]{3,2,1,0:T(8,128)S(1)}, u32[]{:S(2)}, u32[]{:S(2)}) collective-permute-start(f32[3,12,12,1]{3,2,1,0:T(8,128)S(1)} %get-tuple-element.97), channel_id=1, source_target_pairs={{0,1},{1,2},{2,3},{4,5},{5,6},{6,7},{8,9},{9,10},{10,11},{12,13},{... | collective-permute-start | bytes 5192 | tf_op jit(solution)/shard_map/ppermute | solution.py:31
  476.9 9.2 %collective-permute-start.35 = (f32[3,12,12,1]{3,2,1,0:T(8,128)S(1)}, f32[3,12,12,1]{3,2,1,0:T(8,128)S(1)}, u32[]{:S(2)}, u32[]{:S(2)}) collective-permute-start(f32[3,12,12,1]{3,2,1,0:T(8,128)S(1)} %get-tuple-element.98), channel_id=1, source_target_pairs={{1,0},{2,1},{3,2},{5,4},{6,5},{7,6},{9,8},{10,9},{11,10},{13,12},{... | collective-permute-start | bytes 5192 | tf_op jit(solution)/shard_map/ppermute | solution.py:32
  565.2 6.5 collective-permute-start.36
  570.4 8.3 %collective-permute-start.37 = (f32[3,1,8,128]{3,2,1,0:T(8,128)S(1)}, f32[3,1,8,128]{3,2,1,0:T(8,128)S(1)}, u32[]{:S(2)}, u32[]{:S(2)}) collective-permute-start(f32[3,1,8,128]{3,2,1,0:T(8,128)S(1)} %get-tuple-element.266), channel_id=1, source_target_pairs={{32,0},{64,32},{96,64},{128,96},{160,128},{192,160},{224,192},{33,... | collective-permute-start | bytes 36872 | tf_op jit(solution)/shard_map/ppermute | solution.py:32
  578.8 5.6 collective-permute-start.38
  582.5 5.0 collective-permute-start.39
  587.7 12.7 %collective-permute-start.40 = (f32[3,10,10,1]{3,0,2,1:T(4,128)S(1)}, f32[3,10,10,1]{3,0,2,1:T(4,128)S(1)}, u32[]{:S(2)}, u32[]{:S(2)}) collective-permute-start(f32[3,10,10,1]{3,0,2,1:T(4,128)S(1)} %get-tuple-element.235), channel_id=1, source_target_pairs={{0,1},{1,2},{2,3},{4,5},{5,6},{6,7},{8,9},{9,10},{10,11},{12,13},{... | collective-permute-start | bytes 3608 | tf_op jit(solution)/shard_map/ppermute | solution.py:31
  590.1 7.5 %collective-permute-start.41 = (f32[3,10,10,1]{3,0,2,1:T(4,128)S(1)}, f32[3,10,10,1]{3,0,2,1:T(4,128)S(1)}, u32[]{:S(2)}, u32[]{:S(2)}) collective-permute-start(f32[3,10,10,1]{3,0,2,1:T(4,128)S(1)} %get-tuple-element.236), channel_id=1, source_target_pairs={{1,0},{2,1},{3,2},{5,4},{6,5},{7,6},{9,8},{10,9},{11,10},{13,12},{... | collective-permute-start | bytes 3608 | tf_op jit(solution)/shard_map/ppermute | solution.py:32
  (124 other events, 1158.8 us)
where the time goes:
time: 690 us; the launch traced here: 683 us
  blocking collectives  380 us (55%)
  starting transfers between devices  120 us (17%)
  waiting for transfers between devices  85.4 us (12%)
  other arithmetic  64 us (9%)
  local copies, waits for them, and re-layouts  16 us (2%)
  matrix products  9.04 us (1%)
  between operations  7.75 us (1%)
    psum x3, blocking collectives, global_sum(): return lax.psum(value, ('gx', 'gy', 'gz'))  223 us
    unnamed x2, blocking collectives  157 us
    ppermute x21, starting transfers between devices, extended(): before = lax.ppermute(last, axis, up)  87.8 us
    ppermute x21, waiting for transfers between devices, extended(): after = lax.ppermute(leading, axis, down)  76 us
    ppermute x21, starting transfers between devices, extended(): after = lax.ppermute(leading, axis, down)  32.7 us
    another operation x18, other arithmetic, spring_force(): return jnp.stack(parts)  32.1 us
    concatenate x27, other arithmetic, extended(): x = jnp.concatenate([before, x, after], axis=dim)  15.2 us
  transfers between devices with their start and end apart: 42, of which 21 were waited for; matrix products, arithmetic and copies ran while one was open for 4% of the time, Pallas kernels for 0%

commit v1 on v0

v1 whole, which is shorter than its diff:
```python
import functools

import jax
import jax.numpy as jnp
import numpy as np
from jax import lax
from jax.experimental import pallas as pl
from jax.experimental.pallas import tpu as pltpu
from jax.sharding import PartitionSpec as P

MESH = pl.DeviceIdType.MESH
HIGH = lax.Precision.HIGHEST
F32 = jnp.float32

RELAX = 0.6
SWEEPS = 4
SIDE = 8
STRIDE = 11
LEAD = 8
ZH = 2
NODES = 6
MODES = 36


def bond(d):
    return d[0] * d[0] + d[1] * d[1] + d[2] * d[2]


def coef(m, k, d):
    n = bond(d)
    if n == 0:
        return 0.0
    return (1.0 / n if m == k else 0.0) + 0.5 * d[m] * d[k] / (n * n)


def plan(cz):
    rows = -(-(cz + 3) // 8) * 8
    srows = -(-(cz // 2 + 2) // 8) * 8
    total = -(-(3 * rows + srows) // 80) * 80
    return rows, srows, total


def tables(cz):
    rows, srows, total = plan(cz)
    place = np.zeros((64, 128), np.float32)
    for i in range(SIDE):
        for j in range(SIDE):
            place[i * SIDE + j, STRIDE * (i + 1) + j + 1] = 1.0
    spot = {-1: 0, 0: 1, 1: 2, 2: 3, 3: 8, 4: 9}
    place_blocks = np.zeros((16, 128), np.float32)
    for i in range(4):
        for j in range(4):
            place_blocks[i * 4 + j, STRIDE * spot[i] + spot[j]] = 1.0

    def lane_of(x, y):
        return STRIDE * spot[x // 2] + spot[y // 2]

    grow = np.zeros((3 * rows, srows), np.float32)
    for r in range(cz + 2):
        z = r - 1
        grow[r, z // 2 + 1] += 1.0
        for dz in (-1, 1):
            grow[rows + r, (z + dz) // 2 + 1] += 1.0
            grow[2 * rows + r, (z + dz) // 2 + 1] += dz
    pairs = ((0, 0), (1, 1), (2, 2), (0, 1), (0, 2), (1, 2))
    w0 = np.zeros((128, 5 * 128))
    ws = np.zeros((128, 4 * 128))
    wd = np.zeros((128, 2 * 128))
    for x in range(-1, 9):
        for y in range(-1, 9):
            out = STRIDE * (x + 1) + y + 1
            w0[lane_of(x, y), out] += 1.0
            for at, (m, k) in enumerate(pairs):
                if at < 3:
                    whole = sum(
                        coef(m, k, (a, b, c)) for a in (-1, 0, 1) for b in (-1, 0, 1) for c in (-1, 0, 1)
                    )
                    w0[lane_of(x, y), 128 * (at + 1) + out] += 0.5 * whole
                for a in (-1, 0, 1):
                    for b in (-1, 0, 1):
                        src = lane_of(x + a, y + b)
                        if at < 4:
                            w0[src, 128 * (at + 1) + out] += 0.5 * coef(m, k, (a, b, 0))
                            ws[src, 128 * at + out] += 0.5 * coef(m, k, (a, b, 1))
                        else:
                            wd[src, 128 * (at - 4) + out] += 0.5 * coef(m, k, (a, b, 1))
    lane = np.arange(128)
    ints = np.zeros((24, 128), np.int32)
    ints[0:8] = np.where(lane < 110, lane // STRIDE, 99)
    ints[8:16] = np.where(lane < 110, lane % STRIDE, 99)
    ints[16:24] = np.where(lane < 126, lane // 21, 99)
    floats = np.zeros((16, 128), np.float32)
    floats[0:8] = (2.0 * (lane // STRIDE - 1) + 1.0) / SIDE - 1.0
    floats[8:16] = (2.0 * (lane % STRIDE - 1) + 1.0) / SIDE - 1.0
    as32 = lambda a: jnp.asarray(a, F32)
    return (
        as32(place),
        as32(place_blocks),
        as32(grow),
        as32(w0),
        as32(ws),
        as32(wd),
        jnp.asarray(ints),
        as32(floats),
    )


def turn(x, shift):
    shift = shift % 128
    return x if shift == 0 else pltpu.roll(x, shift, 1)


def add_all(items):
    items = list(items)
    while len(items) > 1:
        items = [
            items[i] + items[i + 1] if i + 1 < len(items) else items[i] for i in range(0, len(items), 2)
        ]
    return items[0]


def kernel(
    sizes,
    cz,
    rhs,
    labels,
    moduli,
    nodes_in,
    inverse,
    place,
    place_blocks,
    grow,
    w0,
    ws,
    wd,
    ints,
    floats,
    sol_out,
    res_out,
    mat,
    field,
    zfield,
    qfield,
    rfield,
    pfield,
    vf,
    wf,
    syv,
    dyv,
    syw,
    dyw,
    dmat,
    stiff,
    cdiag,
    node,
    gridm,
    stage,
    rowm,
    ybuf,
    cvec,
    zsend,
    zrecv,
    ysend,
    yrecv,
    xsend,
    xrecv,
    gmsg,
    g1,
    g1c,
    g2,
    mat_sem,
    halo_ss,
    halo_rs,
    g1_ss,
    g1_rs,
    g2_ss,
    g2_rs,
):
    ngx, ngy, ngz = sizes
    rows, srows, total = plan(cz)
    tiles = rows // 8
    sbase = LEAD + 3 * rows
    gx, gy, gz = lax.axis_index("gx"), lax.axis_index("gy"), lax.axis_index("gz")
    zhi, yhi = lax.rem(gx, ZH), lax.div(gx, ZH)
    nline = ZH * ngy
    nplane = (ngx // ZH) * ngz
    slot1 = zhi * ngy + gy
    slot2 = yhi * ngz + gz

    def line_peer(step):
        other = lax.rem(slot1 + step, nline)
        return (yhi * ZH + lax.div(other, ngy), lax.rem(other, ngy), gz)

    def plane_peer(step):
        other = lax.rem(slot2 + step, nplane)
        return (lax.div(other, ngz) * ZH + zhi, gy, lax.rem(other, ngz))

    sides = (
        (gz > 0, (gx, gy, gz - 1)),
        (gz < ngz - 1, (gx, gy, gz + 1)),
        (gy > 0, (gx, gy - 1, gz)),
        (gy < ngy - 1, (gx, gy + 1, gz)),
        (gx > 0, (gx - 1, gy, gz)),
        (gx < ngx - 1, (gx + 1, gy, gz)),
    )

    barrier = pltpu.get_barrier_semaphore()
    for has, device in sides:

        @pl.when(has)
        def _(device=device):
            pl.semaphore_signal(barrier, inc=1, device_id=device, device_id_type=MESH)

    for step in range(1, nline):
        pl.semaphore_signal(barrier, inc=1, device_id=line_peer(step), device_id_type=MESH)
    for step in range(1, nplane):
        pl.semaphore_signal(barrier, inc=1, device_id=plane_peer(step), device_id_type=MESH)

    mat_copy = pltpu.make_async_copy(inverse, mat, mat_sem)
    mat_copy.start()

    lane_x, lane_y, lane_c = ints[0:8, :], ints[8:16, :], ints[16:24, :]
    lane = lax.broadcasted_iota(jnp.int32, (8, 128), 1)
    sub = lax.broadcasted_iota(jnp.int32, (8, 128), 0)
    xi_x, xi_y = floats[0:8, :], floats[8:16, :]

    def base_of(k, i):
        return pl.multiple_of(LEAD + k * rows + 8 * i, 8)

    def xi_z(i):
        along = (sub + (8 * i - 1)).astype(F32)
        return (2.0 * along + 1.0) / cz - 1.0

    for ref in (field, zfield, qfield, rfield, pfield):
        ref[...] = jnp.zeros(ref.shape, F32)
    for ref in (vf, wf, syv, dyv, syw, dyw):
        ref[0:LEAD, :] = jnp.zeros((LEAD, 128), F32)
        ref[LEAD + 3 * rows : LEAD + 3 * rows + 8, :] = jnp.zeros((8, 128), F32)
    node[...] = jnp.zeros(node.shape, F32)
    rowm[...] = jnp.zeros(rowm.shape, F32)
    zsend[...] = jnp.zeros(zsend.shape, F32)
    cvec[...] = jnp.zeros(cvec.shape, F32)
    stage[...] = jnp.zeros(stage.shape, F32)
    for side, (has, _) in enumerate(sides):

        @pl.when(jnp.logical_not(has))
        def _(side=side):
            ref = (zrecv, yrecv, xrecv)[side // 2]
            for t in range(4):
                ref[t, side % 2] = jnp.zeros(ref.shape[2:], F32)

    def across(a, b):
        return lax.dot_general(a, b, (((0,), (0,)), ((), ())), precision=HIGH, preferred_element_type=F32)

    def times(a, b):
        return lax.dot_general(a, b, (((1,), (0,)), ((), ())), precision=HIGH, preferred_element_type=F32)

    def times_t(a, b):
        return lax.dot_general(a, b, (((1,), (1,)), ((), ())), precision=HIGH, preferred_element_type=F32)

    for k in range(3):
        piece = across(rhs[64 * k : 64 * k + 64, :], place[...])
        first = LEAD + k * rows + 1
        field[first : first + cz, :] = piece
        rfield[first : first + cz, :] = piece
    node[1 : 1 + cz, :] = across(nodes_in[...].astype(F32) + 1.0, place[...])
    for i in range(4):
        lab = labels[i]
        value = jnp.zeros(lab.shape, F32)
        for phase in range(moduli.shape[0]):
            value = jnp.where(lab == phase, moduli[phase], value)
        stage[4 * i : 4 * i + 4, :] = value
    blocks = across(stage[...], place_blocks[...])
    field[sbase + 1 : sbase + 1 + cz // 2, :] = blocks

    bad_lane = (
        ((gx == 0) & (lane_x == 0))
        | ((gx == ngx - 1) & (lane_x == 9))
        | ((gy == 0) & (lane_y == 0))
        | ((gy == ngy - 1) & (lane_y == 9))
        | (lane_x > 9)
        | (lane_y > 9)
    )
    low = jnp.where(gz == 0, 1, 0)
    high = jnp.where(gz == ngz - 1, cz + 1, cz + 2)

    def grid_tile(i, carry):
        r = sub + 8 * i
        gridm[pl.ds(pl.multiple_of(8 * i, 8), 8), :] = jnp.where(bad_lane | (r < low) | (r >= high), 0.0, 1.0)
        return carry

    lax.fori_loop(0, tiles, grid_tile, 0)

    def halo(which, side, ref_s, ref_r):
        return pltpu.make_async_remote_copy(
            src_ref=ref_s.at[which, side % 2],
            dst_ref=ref_r.at[which, 1 - side % 2],
            send_sem=halo_ss.at[which, side],
            recv_sem=halo_rs.at[which, side + 1 - 2 * (side % 2)],
            device_id=sides[side][1],
            device_id_type=MESH,
        )

    def start(which, axis, ref_s, ref_r):
        for side in (2 * axis, 2 * axis + 1):

            @pl.when(sides[side][0])
            def _(side=side):
                halo(which, side, ref_s, ref_r).start()

    def arrive(which, axis, ref_s, ref_r):
        for side in (2 * axis, 2 * axis + 1):

            @pl.when(sides[side][0])
            def _(side=side):
                pltpu.make_async_remote_copy(
                    src_ref=ref_s.at[which, side % 2],
                    dst_ref=ref_r.at[which, side % 2],
                    send_sem=halo_ss.at[which, side],
                    recv_sem=halo_rs.at[which, side],
                    device_id=sides[side][1],
                    device_id_type=MESH,
                ).wait_recv()

    def left(which, axis, ref_s, ref_r):
        for side in (2 * axis, 2 * axis + 1):

            @pl.when(sides[side][0])
            def _(side=side):
                halo(which, side, ref_s, ref_r).wait_send()

    def z_rows(width):
        if width == 1:
            got = [(LEAD + k * rows, cz, k) for k in range(3)] + [(sbase, cz // 2, 3)]
            return [(r + n, r + 1, r, r + n + 1, at) for r, n, at in got]
        out = []
        for k in range(3):
            for layer in range(2):
                r = LEAD + k * rows + layer
                out.append((r + cz, r, r, r + cz, 2 * k + layer))
        return out

    def pack_z(ref, which, width):
        for up_from, down_from, _, _, at in z_rows(width):
            zsend[which, 0, at : at + 1, :] = ref[down_from : down_from + 1, :]
            zsend[which, 1, at : at + 1, :] = ref[up_from : up_from + 1, :]

    def unpack_z(ref, which, width):
        for _, _, low_to, high_to, at in z_rows(width):
            ref[low_to : low_to + 1, :] += zrecv[which, 0, at : at + 1, :]
            ref[high_to : high_to + 1, :] += zrecv[which, 1, at : at + 1, :]

    def scheme(axis, width):
        if width == 1:
            if axis == 1:
                return 10, total // 80, lambda k: lane_y == k, lambda k: (k - 1, k - 8), (lane_y == 0, lane_y == 9), lambda k: (-k, 9 - k)
            return (
                10,
                total // 80,
                lambda k: lane_x == k,
                lambda k: (STRIDE * (k - 1), STRIDE * (k - 8)),
                (lane_x == 0, lane_x == 9),
                lambda k: (-STRIDE * k, STRIDE * (9 - k)),
            )
        if axis == 1:
            return (
                5,
                -(-3 * rows // 40),
                lambda k: (lane_y == 2 * k) | (lane_y == 2 * k + 1),
                lambda k: (2 * k, 2 * k - 8),
                (lane_y < 2, (lane_y == 8) | (lane_y == 9)),
                lambda k: (-2 * k, 8 - 2 * k),
            )
        return (
            6,
            -(-3 * rows // 48),
            lambda k: lane_c == k,
            lambda k: (21 * k, 21 * k - 88),
            (lane < 21, (lane >= 88) & (lane < 109)),
            lambda k: (-21 * k, 88 - 21 * k),
        )

    def pack(ref, which, axis, width, buf):
        chunks, deep, mask, shift, _, _ = scheme(axis, width)
        masks = [mask(k) for k in range(chunks)]

        def one(t, carry):
            down, up = jnp.zeros((8, 128), F32), jnp.zeros((8, 128), F32)
            for k in range(chunks):
                tile = ref[pl.ds(pl.multiple_of(LEAD + 8 * (k * deep + t), 8), 8), :]
                down = jnp.where(masks[k], turn(tile, shift(k)[0]), down)
                up = jnp.where(masks[k], turn(tile, shift(k)[1]), up)
            at = pl.ds(pl.multiple_of(8 * t, 8), 8)
            buf[which, 0, at, :] = down
            buf[which, 1, at, :] = up
            return carry

        lax.fori_loop(0, deep, one, 0)

    def unpack(ref, which, axis, width, buf):
        chunks, deep, _, _, ends, shift = scheme(axis, width)

        def one(t, carry):
            at = pl.ds(pl.multiple_of(8 * t, 8), 8)
            from_low, from_high = buf[which, 0, at, :], buf[which, 1, at, :]
            for k in range(chunks):
                rows_k = pl.ds(pl.multiple_of(LEAD + 8 * (k * deep + t), 8), 8)
                tile = ref[rows_k, :]
                tile = tile + jnp.where(ends[0], turn(from_low, shift(k)[0]), 0.0)
                tile = tile + jnp.where(ends[1], turn(from_high, shift(k)[1]), 0.0)
                ref[rows_k, :] = tile
            return carry

        lax.fori_loop(0, deep, one, 0)

    def cut(ref, axis, width):
        deep = 8 * scheme(axis, width)[1]
        return ref.at[:, :, 0:deep, :]

    def exchange(ref, which, width, between=None):
        pack_z(ref, which, width)
        start(which, 0, zsend, zrecv)
        arrive(which, 0, zsend, zrecv)
        unpack_z(ref, which, width)
        pack(ref, which, 1, width, ysend)
        start(which, 1, cut(ysend, 1, width), cut(yrecv, 1, width))
        arrive(which, 1, cut(ysend, 1, width), cut(yrecv, 1, width))
        unpack(ref, which, 1, width, yrecv)
        pack(ref, which, 2, width, xsend)
        start(which, 2, cut(xsend, 2, width), cut(xrecv, 2, width))
        if between is not None:
            between()
        arrive(which, 2, cut(xsend, 2, width), cut(xrecv, 2, width))
        unpack(ref, which, 2, width, xrecv)

    def line_copy(which, step):
        return pltpu.make_async_remote_copy(
            src_ref=gmsg.at[which, pl.ds(0, 1)],
            dst_ref=g1.at[which, pl.ds(slot1, 1)],
            send_sem=g1_ss.at[which, step],
            recv_sem=g1_rs.at[which, slot1],
            device_id=line_peer(step),
            device_id_type=MESH,
        )

    def line_start(which, message):
        gmsg[which] = message
        g1[which, pl.ds(slot1, 1), :] = message[0:1, :]
        for step in range(1, nline):
            line_copy(which, step).start()

    def line_arrive(which):
        for step in range(1, nline):
            other = lax.rem(slot1 + step, nline)
            pltpu.make_async_remote_copy(
                src_ref=gmsg.at[which, pl.ds(0, 1)],
                dst_ref=g1.at[which, pl.ds(other, 1)],
                send_sem=g1_ss.at[which, step],
                recv_sem=g1_rs.at[which, other],
                device_id=line_peer(step),
                device_id_type=MESH,
            ).wait_recv()

    def plane_copy(which, step):
        return pltpu.make_async_remote_copy(
            src_ref=g1c.at[which],
            dst_ref=g2.at[which, slot2],
            send_sem=g2_ss.at[which, step],
            recv_sem=g2_rs.at[which, slot2],
            device_id=plane_peer(step),
            device_id_type=MESH,
        )

    def plane_start(which, block):
        g1c[which] = block
        g2[which, pl.ds(slot2, 1)] = block[None]
        for step in range(1, nplane):
            plane_copy(which, step).start()

    def plane_arrive(which):
        for step in range(1, nplane):
            other = lax.rem(slot2 + step, nplane)
            pltpu.make_async_remote_copy(
                src_ref=g1c.at[which],
                dst_ref=g2.at[which, other],
                send_sem=g2_ss.at[which, step],
                recv_sem=g2_rs.at[which, other],
                device_id=plane_peer(step),
                device_id_type=MESH,
            ).wait_recv()

    def moments(ref):
        def one(i, acc):
            r = [ref[pl.ds(base_of(k, i), 8), :] for k in range(3)]
            own = node[pl.ds(pl.multiple_of(8 * i, 8), 8), :]
            z = xi_z(i)
            parts = r + [xi_y * r[2] - z * r[1], z * r[0] - xi_x * r[2], xi_x * r[1] - xi_y * r[0]]
            out = []
            for g in range(NODES):
                here = own == float(g + 1)
                for m in range(6):
                    out.append(acc[6 * g + m] + jnp.where(here, parts[m], 0.0))
            return tuple(out)

        acc = lax.fori_loop(0, tiles, one, tuple(jnp.zeros((8, 128), F32) for _ in range(MODES)))
        for at in range(MODES):
            rowm[at : at + 1, :] = jnp.sum(acc[at], axis=0, keepdims=True)

    def row_to_lanes():
        return times_t(jnp.ones((8, 128), F32), rowm[...])

    turned = lax.rem((gy * ngz + gz) * MODES, 128)

    def own_range(c):
        begin = (sub * ngz + c) * MODES - 128 * sub
        ahead = begin < 128
        first = (lane >= begin) & (lane < begin + MODES)
        second = (lane + 128 >= begin) & (lane + 128 < begin + MODES)
        return first, second

    def coarse_solve(which):
        ranges = [own_range(c) for c in range(ngz)]
        acc = [jnp.zeros((8, 128), F32) for _ in range(5)]
        for y in range(ngx // ZH):
            for h in range(ZH):
                a = y * ZH + h
                got = [g2[which, y * ngz + c, 8 * h : 8 * h + 8, :] for c in range(ngz)]
                main = add_all([jnp.where(ranges[c][0], got[c], 0.0) for c in range(ngz)])
                nxt = add_all([jnp.where(ranges[c][1], got[c], 0.0) for c in range(ngz)])
                cvec[16 * a + 8 : 16 * a + 9, :] = jnp.zeros((1, 128), F32)
                cvec[16 * a : 16 * a + 8, :] = main
                cvec[16 * a + 1 : 16 * a + 9, :] += nxt
        for a in range(ngx):
            for j in range(9):
                row = jnp.broadcast_to(cvec[16 * a + j : 16 * a + j + 1, :], (8, 128))
                col = 128 * (9 * a + j)
                for t in range(4):
                    acc[t] = acc[t] + mat[8 * t : 8 * t + 8, col : col + 128] * row
                acc[4] = acc[4] + jnp.concatenate([mat[32:36, col : col + 128]] * 2, axis=0) * row
        for t in range(5):
            ybuf[8 * t : 8 * t + 8, :] = jnp.broadcast_to(jnp.sum(acc[t], axis=1, keepdims=True), (8, 128))

    def lane_sum(which, at):
        parts = []
        for c in range(ngz):
            pos = lax.rem((sub * ngz + c) * MODES + at, 128)
            here = lane == pos
            for y in range(ngx // ZH):
                for h in range(ZH):
                    parts.append(jnp.where(here, g2[which, y * ngz + c, 8 * h : 8 * h + 8, :], 0.0))
        whole = jnp.sum(add_all(parts), axis=0, keepdims=True)
        return jnp.sum(whole, axis=1, keepdims=True)

    def with_coarse(src, dst):
        def one(i, carry):
            own = node[pl.ds(pl.multiple_of(8 * i, 8), 8), :]
            grid = gridm[pl.ds(pl.multiple_of(8 * i, 8), 8), :]
            z = xi_z(i)
            modes = [jnp.zeros((8, 128), F32) for _ in range(6)]
            for g in range(NODES):
                here = own == float(g + 1)
                for m in range(6):
                    at = 6 * g + m
                    modes[m] = jnp.where(here, jnp.broadcast_to(ybuf[at : at + 1, :], (8, 128)), modes[m])
            t, w = modes[:3], modes[3:]
            add = [
                t[0] + (w[1] * z - w[2] * xi_y),
                t[1] + (w[2] * xi_x - w[0] * z),
                t[2] + (w[0] * xi_y - w[1] * xi_x),
            ]
            for k in range(3):
                at = pl.ds(base_of(k, i), 8)
                dst[at, :] = src[at, :] * grid + add[k]
            return carry

        lax.fori_loop(0, tiles, one, 0)

    def spread(ref):
        def one(i, carry):
            s = stiff[pl.ds(pl.multiple_of(8 * i, 8), 8), :]
            for k in range(3):
                at = pl.ds(base_of(k, i), 8)
                v = ref[at, :]
                w = s * v
                vf[at, :] = v
                wf[at, :] = w
                for x, sy, dy in ((v, syv, dyv), (w, syw, dyw)):
                    ahead, behind = turn(x, -1), turn(x, 1)
                    sy[at, :] = ahead + behind
                    dy[at, :] = ahead - behind
            return carry

        lax.fori_loop(0, tiles, one, 0)

    def couple(u_ref, sy_ref, dy_ref, i):
        def at(ref, k, dz):
            return ref[pl.ds(base_of(k, i) + dz, 8), :]

        up = [at(u_ref, k, 1) for k in range(3)]
        um = [at(u_ref, k, -1) for k in range(3)]
        u = [at(u_ref, k, 0) for k in range(3)]
        s = [up[k] + um[k] for k in range(3)]
        yp = [at(sy_ref, k, 1) for k in range(3)]
        ym = [at(sy_ref, k, -1) for k in range(3)]
        sy = [at(sy_ref, k, 0) for k in range(3)]
        sys = [yp[k] + ym[k] for k in range(3)]
        t_x, t_z = up[0] - um[0], up[2] - um[2]
        ty_x, ty_z = yp[0] - ym[0], yp[2] - ym[2]
        dp = [at(dy_ref, k, 1) for k in range(3)]
        dm = [at(dy_ref, k, -1) for k in range(3)]
        dys_x, dys_y = dp[0] + dm[0], dp[1] + dm[1]
        dyt_y, dyt_z = dp[1] - dm[1], dp[2] - dm[2]
        dy_x, dy_y = at(dy_ref, 0, 0), at(dy_ref, 1, 0)
        e, th, c7 = 0.125, 1.0 / 18.0, 7.0 / 18.0
        still = [
            sy[0] + s[0] + 0.5 * sys[0],
            1.5 * sy[1] + s[1] + 0.625 * sys[1] + e * dyt_z,
            sy[2] + 1.5 * s[2] + 0.625 * sys[2] + e * dyt_y,
        ]
        even = [
            1.5 * u[0] + 0.625 * (sy[0] + s[0]) + c7 * sys[0],
            u[1] + 0.625 * sy[1] + 0.5 * s[1] + c7 * sys[1] + th * dyt_z,
            u[2] + 0.5 * sy[2] + 0.625 * s[2] + c7 * sys[2] + th * dyt_y,
        ]
        odd = [
            e * (dy_y + t_z) + th * (dys_y + ty_z),
            e * dy_x + th * dys_x,
            e * t_x + th * ty_x,
        ]
        return [
            still[k] + (turn(even[k] + odd[k], -STRIDE) + turn(even[k] - odd[k], STRIDE)) for k in range(3)
        ], u

    def image_tile(i):
        here = pl.ds(pl.multiple_of(8 * i, 8), 8)
        lv, v = couple(vf, syv, dyv, i)
        lw, _ = couple(wf, syw, dyw, i)
        s = stiff[here, :]
        d = [dmat[pl.ds(pl.multiple_of(rows * f + 8 * i, 8), 8), :] for f in range(6)]
        full = ((0, 3, 4), (3, 1, 5), (4, 5, 2))
        out = []
        for m in range(3):
            diag = d[full[m][0]] * v[0] + d[full[m][1]] * v[1] + d[full[m][2]] * v[2]
            out.append(diag - 0.5 * (s * lv[m] + lw[m]))
        return out, v

    def local_solve(ref, out):
        def first(i, carry):
            for k in range(3):
                at = pl.ds(base_of(k, i), 8)
                out[at, :] = cdiag[pl.ds(pl.multiple_of(rows * k + 8 * i, 8), 8), :] * ref[at, :]
            return carry

        lax.fori_loop(0, tiles, first, 0)

        def sweep(n, carry):
            spread(out)

            def one(i, inner):
                image, v = image_tile(i)
                for k in range(3):
                    at = pl.ds(base_of(k, i), 8)
                    c = cdiag[pl.ds(pl.multiple_of(rows * k + 8 * i, 8), 8), :]
                    out[at, :] = v[k] + c * (ref[at, :] - image[k])
                return inner

            lax.fori_loop(0, tiles, one, 0)
            return carry

        lax.fori_loop(0, SWEEPS - 1, sweep, 0)

    def setup_stiffness():
        blocks_all = field[sbase : sbase + srows, :]
        fine = times(grow[...], blocks_all)
        flat, both, tilt = fine[0:rows], fine[rows : 2 * rows], fine[2 * rows : 3 * rows]
        for f in range(7):
            total_f = None
            if f < 5:
                total_f = times(flat, w0[:, 128 * f : 128 * f + 128])
            if 1 <= f < 5:
                total_f = total_f + times(both, ws[:, 128 * (f - 1) : 128 * f])
            if f >= 5:
                total_f = times(tilt, wd[:, 128 * (f - 5) : 128 * (f - 4)])
            if f == 0:
                stiff[...] = total_f
            else:
                dmat[rows * (f - 1) : rows * f, :] = total_f
        r = lax.broadcasted_iota(jnp.int32, (rows, 128), 0)
        for k in range(3):
            d = dmat[rows * k : rows * k + rows, :]
            live = (r < cz + 2) & (d > 0.0)
            cdiag[rows * k : rows * k + rows, :] = jnp.where(live, RELAX / jnp.where(live, d, 1.0), 0.0)

    moments(field)
    first_row = turn_by(row_to_lanes(), turned)
    greeters = nline - 1 + nplane - 1
    for has, _ in sides:
        greeters = greeters + jnp.where(has, 1, 0)
    pl.semaphore_wait(barrier, greeters)

    def forward(which):
        def run():
            line_arrive(which)
            plane_start(which, g1[which])

        return run

    line_start(0, first_row)
    exchange(field, 0, 1, forward(0))
    setup_stiffness()
    local_solve(field, pfield)
    mat_copy.wait()
    plane_arrive(0)
    coarse_solve(0)
    with_coarse(pfield, zfield)
    exchange(zfield, 1, 2)

    spread(zfield)

    def image_and_sums(dst, first, second):
        def one(i, acc):
            image, v = image_tile(i)
            own = node[pl.ds(pl.multiple_of(8 * i, 8), 8), :] > 0.0
            acc = list(acc)
            for k in range(3):
                at = pl.ds(base_of(k, i), 8)
                mine = jnp.where(own, image[k], 0.0)
                dst[at, :] = mine
                acc[0] = acc[0] + first[at, :] * v[k]
                acc[1] = acc[1] + v[k] * mine
                if second is not None:
                    acc[2] = acc[2] + second[at, :] * v[k]
            return tuple(acc)

        count = 2 if second is None else 3
        acc = lax.fori_loop(0, tiles, one, tuple(jnp.zeros((8, 128), F32) for _ in range(count)))
        return [jnp.sum(a, axis=0, keepdims=True) for a in acc]

    sums = image_and_sums(qfield, rfield, None)
    moments(qfield)
    rowm[MODES : MODES + 1, :] = sums[0]
    rowm[MODES + 1 : MODES + 2, :] = sums[1]
    second_row = turn_by(row_to_lanes(), turned)

    line_start(1, second_row)
    for k in range(3):
        field[LEAD + rows * k : LEAD + rows * (k + 1), :] = qfield[LEAD + rows * k : LEAD + rows * (k + 1), :]
    exchange(field, 2, 1, forward(1))
    local_solve(field, pfield)
    plane_arrive(1)
    coarse_solve(1)
    rho0 = lane_sum(1, MODES)
    curve0 = lane_sum(1, MODES + 1)
    alpha0 = rho0 / curve0
    with_coarse(pfield, field)
    exchange(field, 3, 2)

    def renew(i, carry):
        for k in range(3):
            at = pl.ds(base_of(k, i), 8)
            field[at, :] = zfield[at, :] - alpha0 * field[at, :]
            rfield[at, :] = rfield[at, :] - alpha0 * qfield[at, :]
        return carry

    lax.fori_loop(0, tiles, renew, 0)
    spread(field)

    sums = image_and_sums(pfield, rfield, qfield)
    rowm[0:MODES, :] = jnp.zeros((MODES, 128), F32)
    for at in range(3):
        rowm[MODES + at : MODES + at + 1, :] = sums[at]
    line_start(2, turn_by(row_to_lanes(), turned))
    line_arrive(2)
    plane_start(2, g1[2])
    plane_arrive(2)
    rho1 = lane_sum(2, MODES)
    zaz = lane_sum(2, MODES + 1)
    zq = lane_sum(2, MODES + 2)
    beta = rho1 / rho0
    alpha1 = rho1 / (zaz + 2.0 * beta * zq + beta * beta * curve0)

    for k in range(3):
        at = slice(LEAD + k * rows + 1, LEAD + k * rows + 1 + cz)
        z0, z1 = zfield[at, :], field[at, :]
        sol_out[64 * k : 64 * k + 64, :] = times_t(place[...], alpha0 * z0 + alpha1 * (z1 + beta * z0))
        res_out[64 * k : 64 * k + 64, :] = times_t(
            place[...], rfield[at, :] - alpha1 * (pfield[at, :] + beta * qfield[at, :])
        )

    for which in range(4):
        width = 1 + which % 2
        left(which, 0, zsend, zrecv)
        left(which, 1, cut(ysend, 1, width), cut(yrecv, 1, width))
        left(which, 2, cut(xsend, 2, width), cut(xrecv, 2, width))
    for which in range(3):
        for step in range(1, nline):
            line_copy(which, step).wait_send()
        for step in range(1, nplane):
            plane_copy(which, step).wait_send()


def turn_by(x, shift):
    return pltpu.roll(x, shift, 1)


def solution(mesh):
    sizes = (mesh.shape["gx"], mesh.shape["gy"], mesh.shape["gz"])
    nline = ZH * sizes[1]
    nplane = (sizes[0] // ZH) * sizes[2]

    def body(right_side, phase_labels, phase_moduli, coarse_nodes, coarse_inverse):
        cz = right_side.shape[3]
        rows, srows, total = plan(cz)
        tall = pltpu.VMEM((LEAD + total, 128), F32)
        ydeep = max(total // 10, 8 * -(-3 * rows // 40))
        xdeep = max(total // 10, 8 * -(-3 * rows // 48))
        vmem = pl.BlockSpec(memory_space=pltpu.VMEM)
        consts = tables(cz)
        sol, res = pl.pallas_call(
            functools.partial(kernel, sizes, cz),
            out_shape=(jax.ShapeDtypeStruct((192, cz), F32),) * 2,
            in_specs=[
                vmem,
                vmem,
                pl.BlockSpec(memory_space=pltpu.SMEM),
                vmem,
                pl.BlockSpec(memory_space=pl.ANY),
            ]
            + [vmem] * len(consts),
            out_specs=(vmem, vmem),
            scratch_shapes=[
                pltpu.VMEM(coarse_inverse.shape, F32),
                tall,
                tall,
                tall,
                tall,
                tall,
                tall,
                tall,
                tall,
                tall,
                tall,
                tall,
                pltpu.VMEM((6 * rows, 128), F32),
                pltpu.VMEM((rows, 128), F32),
                pltpu.VMEM((3 * rows, 128), F32),
                pltpu.VMEM((rows, 128), F32),
                pltpu.VMEM((rows, 128), F32),
                pltpu.VMEM((16, cz // 2), F32),
                pltpu.VMEM((128, 128), F32),
                pltpu.VMEM((40, 128), F32),
                pltpu.VMEM((16 * sizes[0], 128), F32),
                pltpu.VMEM((4, 2, 8, 128), F32),
                pltpu.VMEM((4, 2, 8, 128), F32),
                pltpu.VMEM((4, 2, ydeep, 128), F32),
                pltpu.VMEM((4, 2, ydeep, 128), F32),
                pltpu.VMEM((4, 2, xdeep, 128), F32),
                pltpu.VMEM((4, 2, xdeep, 128), F32),
                pltpu.VMEM((3, 8, 128), F32),
                pltpu.VMEM((3, nline, 128), F32),
                pltpu.VMEM((3, nline, 128), F32),
                pltpu.VMEM((3, nplane, nline, 128), F32),
                pltpu.SemaphoreType.DMA,
                pltpu.SemaphoreType.DMA((4, 6)),
                pltpu.SemaphoreType.DMA((4, 6)),
                pltpu.SemaphoreType.DMA((3, nline)),
                pltpu.SemaphoreType.DMA((3, nline)),
                pltpu.SemaphoreType.DMA((3, nplane)),
                pltpu.SemaphoreType.DMA((3, nplane)),
            ],
            compiler_params=pltpu.CompilerParams(
                collective_id=0, has_side_effects=True, vmem_limit_bytes=48 * 1024 * 1024
            ),
            name="schwarz_cg",
        )(
            right_side.reshape(192, cz),
            phase_labels,
            phase_moduli,
            coarse_nodes.reshape(64, cz),
            coarse_inverse,
            *consts,
        )
        return sol.reshape(right_side.shape), res.reshape(right_side.shape)

    spec = P(None, "gx", "gy", "gz")
    cells = P("gx", "gy", "gz")
    return jax.shard_map(
        body,
        mesh=mesh,
        in_specs=(spec, cells, P(), cells, P(("gx", "gy", "gz"), None)),
        out_specs=(spec, spec),
        check_vma=False,
    )
```

time: 690 us -> 120 us (0.17)
  blocking collectives: 380 us -> 0 us
  starting transfers between devices: 120 us -> 0 us
  Pallas kernels: 0 us -> 107 us
  waiting for transfers between devices: 85.4 us -> 0 us
  other arithmetic: 64 us -> 0 us
  matrix products: 9.04 us -> 0 us
  between operations: 7.75 us -> 0.66 us
    psum x3 -> x0, blocking collectives: 223 us -> none  [global_sum(): return lax.psum(value, ('gx', 'gy', 'gz'))]
    unnamed x2 -> x0, blocking collectives: 157 us -> none
    ppermute x42 -> x0, starting transfers between devices: 120 us -> none  [the longest x21 87.8 us: extended(): before = lax.ppermute(last, axis, up)]
    pallas_call x0 -> x1, Pallas kernels: none -> 107 us  [body(): pl.pallas_call(functools.partial(kernel, sizes, cz), out_shape=(jax.Shape...]
    ppermute x42 -> x0, waiting for transfers between devices: 85.4 us -> none  [the longest x21 76 us: extended(): after = lax.ppermute(leading, axis, down)]
    another operation x21 -> x0, other arithmetic: 33.8 us -> none  [the longest x18 32.1 us: spring_force(): return jnp.stack(parts)]
    concatenate x31 -> x0, other arithmetic: 15.6 us -> none  [the longest x27 15.2 us: extended(): x = jnp.concatenate([before, x, after], axis=dim)]
    dot_general x6 -> x0, matrix products: 9.04 us -> none  [the longest x2 3.86 us: accumulate(): return jnp.dot(coarse_inverse, piece, precision=highest)]
  transfers between devices with their start and end apart: 42 -> 0, of which waited for: 21 -> 0; matrix products, arithmetic and copies ran while one was open for 4% -> 0% of each run, Pallas kernels for 0% -> 0%
where the time goes in v1:
time: 120 us
  Pallas kernels  107 us (89%)
  local copies, waits for them, and re-layouts  12.3 us (10%)
    pallas_call x1, Pallas kernels, body(): pl.pallas_call(functools.partial(kernel, sizes, cz), out_shape=(jax.Shape...  107 us
    unnamed x28, local copies, waits for them, and re-layouts  12.3 us

profile of v1, /device:TPU:1, one launch (start us, length us, event | category | flops | bytes accessed | tf_op | source)
XLA Modules:
  0.0 119.6 jit_solution(5574023343316988928)
XLA Ops:
  0.6 0.0 copy-start
  0.6 1.4 %copy-done = f32[36,9216]{1,0:T(8,128)S(1)} copy-done((f32[36,9216]{1,0:T(8,128)S(1)}, f32[36,9216]{1,0:T(8,128)}, u32[]{:S(2)}) %copy-start) | copy-done | bytes 1327128
  2.0 0.0 copy-start.1
  2.0 1.0 copy-done.1
  3.0 0.0 copy-start.2
  3.0 0.9 copy-done.2
  3.9 0.0 copy-start.3
  3.9 0.9 copy-done.3
  4.9 0.0 copy-start.4
  4.9 0.9 copy-done.4
  5.8 0.0 copy-start.5
  5.8 0.9 copy-done.5
  6.7 0.0 copy-start.6
  6.7 0.8 copy-done.6
  7.4 0.0 copy-start.7
  7.4 0.8 copy-done.7
  8.2 0.0 copy-start.8
  8.2 0.7 copy-done.8
  8.9 0.0 copy-start.9
  8.9 0.7 copy-done.9
  9.6 0.0 copy-start.10
  9.6 0.7 copy-done.10
  10.3 0.0 copy-start.11
  10.3 0.7 copy-done.11
  11.0 0.0 copy-start.12
  11.0 0.7 copy-done.12
  11.6 106.7 %schwarz_cg.1 = (f32[192,128]{1,0:T(8,128)S(1)}, f32[192,128]{1,0:T(8,128)S(1)}) custom-call(f32[192,128]{1,0:T(8,128)S(1)} %bitcast.4, s32[4,4,64]{2,1,0:T(4,128)S(1)} %copy-done.9, f32[8]{0:T(128)S(1)} %copy-done.12, s32[64,128]{1,0:T(8,128)S(1)} %bitcast.7, f32[36,9216]{1,0:T(8,128)S(1)} %copy-done, f32[64,128]{1,0:T(8,128)S(1)} %copy-done.7, ...), custom_call_target="tpu_custom_call" | custom-call | tf_op jit(solution)/shard_map/schwarz_cg/pallas_call | solution.py:819
  118.3 0.6 copy.17
  118.9 0.6 copy.18
Async XLA Ops:
  0.6 1.4 %copy-start = (f32[36,9216]{1,0:T(8,128)S(1)}, f32[36,9216]{1,0:T(8,128)}, u32[]{:S(2)}) copy-start(f32[36,9216]{1,0:T(8,128)} %inverse.1) | copy-start | bytes 3981316
  2.0 1.0 copy-start.1
  3.0 0.9 copy-start.2
  3.9 0.9 copy-start.3
  4.9 0.9 copy-start.4
  5.8 0.9 copy-start.5
  6.7 0.8 copy-start.6
  7.4 0.8 copy-start.7
  8.2 0.7 copy-start.8
  8.9 0.7 copy-start.9
  9.6 0.7 copy-start.10
  10.3 0.7 copy-start.11
  11.0 0.7 copy-start.12

commit v2 on v1

--- a/solution.py
+++ b/solution.py
@@ -55,35 +55,20 @@
     def lane_of(x, y):
         return STRIDE * spot[x // 2] + spot[y // 2]
 
-    grow = np.zeros((3 * rows, srows), np.float32)
-    for r in range(cz + 2):
-        z = r - 1
-        grow[r, z // 2 + 1] += 1.0
-        for dz in (-1, 1):
-            grow[rows + r, (z + dz) // 2 + 1] += 1.0
-            grow[2 * rows + r, (z + dz) // 2 + 1] += dz
     pairs = ((0, 0), (1, 1), (2, 2), (0, 1), (0, 2), (1, 2))
-    w0 = np.zeros((128, 5 * 128))
-    ws = np.zeros((128, 4 * 128))
-    wd = np.zeros((128, 2 * 128))
+    mix = np.zeros((128, 11 * 128))
     for x in range(-1, 9):
         for y in range(-1, 9):
             out = STRIDE * (x + 1) + y + 1
-            w0[lane_of(x, y), out] += 1.0
+            mix[lane_of(x, y), out] += 1.0
             for at, (m, k) in enumerate(pairs):
-                if at < 3:
-                    whole = sum(
-                        coef(m, k, (a, b, c)) for a in (-1, 0, 1) for b in (-1, 0, 1) for c in (-1, 0, 1)
-                    )
-                    w0[lane_of(x, y), 128 * (at + 1) + out] += 0.5 * whole
                 for a in (-1, 0, 1):
                     for b in (-1, 0, 1):
                         src = lane_of(x + a, y + b)
                         if at < 4:
-                            w0[src, 128 * (at + 1) + out] += 0.5 * coef(m, k, (a, b, 0))
-                            ws[src, 128 * at + out] += 0.5 * coef(m, k, (a, b, 1))
-                        else:
-                            wd[src, 128 * (at - 4) + out] += 0.5 * coef(m, k, (a, b, 1))
+                            mix[src, 128 * (1 + at) + out] += 72.0 * coef(m, k, (a, b, 0))
+                        mix[src, 128 * (5 + at) + out] += 72.0 * coef(m, k, (a, b, 1))
+    mix = np.round(mix)
     lane = np.arange(128)
     ints = np.zeros((24, 128), np.int32)
     ints[0:8] = np.where(lane < 110, lane // STRIDE, 99)
@@ -92,17 +77,18 @@
     floats = np.zeros((16, 128), np.float32)
     floats[0:8] = (2.0 * (lane // STRIDE - 1) + 1.0) / SIDE - 1.0
     floats[8:16] = (2.0 * (lane % STRIDE - 1) + 1.0) / SIDE - 1.0
-    as32 = lambda a: jnp.asarray(a, F32)
-    return (
-        as32(place),
-        as32(place_blocks),
-        as32(grow),
-        as32(w0),
-        as32(ws),
-        as32(wd),
-        jnp.asarray(ints),
-        as32(floats),
-    )
+    half = lambda a: jnp.asarray(a, jnp.bfloat16)
+    return half(place), half(place_blocks), half(mix), jnp.asarray(ints), jnp.asarray(floats)
+
+
+WHOLE = sum(coef(0, 0, (a, b, c)) for a in (-1, 0, 1) for b in (-1, 0, 1) for c in (-1, 0, 1))
+
+
+def thirds(x):
+    high = x.astype(jnp.bfloat16)
+    rest = x - high.astype(F32)
+    middle = rest.astype(jnp.bfloat16)
+    return high, middle, (rest - middle.astype(F32)).astype(jnp.bfloat16)
 
 
 def turn(x, shift):
@@ -122,22 +108,28 @@
 def kernel(
     sizes,
     cz,
-    rhs,
-    labels,
+    rhs_hbm,
+    labels_hbm,
     moduli,
-    nodes_in,
+    nodes_hbm,
     inverse,
-    place,
-    place_blocks,
-    grow,
-    w0,
-    ws,
-    wd,
-    ints,
-    floats,
+    place_hbm,
+    place_blocks_hbm,
+    mix_hbm,
+    ints_hbm,
+    floats_hbm,
     sol_out,
     res_out,
     mat,
+    rhs,
+    labels,
+    nodes_in,
+    place,
+    place_blocks,
+    mix,
+    ints,
+    floats,
+    mixed,
     field,
     zfield,
     qfield,
@@ -168,7 +160,7 @@
     g1,
     g1c,
     g2,
-    mat_sem,
+    load_sem,
     halo_ss,
     halo_rs,
     g1_ss,
@@ -216,21 +208,54 @@
     for step in range(1, nplane):
         pl.semaphore_signal(barrier, inc=1, device_id=plane_peer(step), device_id_type=MESH)
 
-    mat_copy = pltpu.make_async_copy(inverse, mat, mat_sem)
-    mat_copy.start()
-
-    lane_x, lane_y, lane_c = ints[0:8, :], ints[8:16, :], ints[16:24, :]
+    loads = [
+        pltpu.make_async_copy(src, dst, load_sem.at[at])
+        for at, (src, dst) in enumerate(
+            (
+                (rhs_hbm, rhs),
+                (nodes_hbm, nodes_in),
+                (labels_hbm, labels),
+                (place_hbm, place),
+                (place_blocks_hbm, place_blocks),
+                (ints_hbm, ints),
+                (floats_hbm, floats),
+                (mix_hbm, mix),
+                (inverse, mat),
+            )
+        )
+    ]
+    for load in loads:
+        load.start()
+    mat_copy, mix_copy = loads[-1], loads[-2]
+
     lane = lax.broadcasted_iota(jnp.int32, (8, 128), 1)
     sub = lax.broadcasted_iota(jnp.int32, (8, 128), 0)
-    xi_x, xi_y = floats[0:8, :], floats[8:16, :]
 
     def base_of(k, i):
-        return pl.multiple_of(LEAD + k * rows + 8 * i, 8)
+        return tile_at(LEAD + k * rows, i)
+
+    def tile_at(first, i):
+        return first + 8 * i if isinstance(i, int) else pl.multiple_of(first + 8 * i, 8)
+
+    def each_tile(one, unroll=4):
+        whole = tiles // unroll
+
+        def some(n, carry):
+            for j in range(unroll):
+                one(n * unroll + j)
+            return carry
+
+        lax.fori_loop(0, whole, some, 0)
+        for i in range(whole * unroll, tiles):
+            one(i)
 
     def xi_z(i):
         along = (sub + (8 * i - 1)).astype(F32)
         return (2.0 * along + 1.0) / cz - 1.0
 
+    for f in range(6):
+        dmat[rows * f + cz + 2 : rows * (f + 1), :] = jnp.zeros((rows - cz - 2, 128), F32)
+    stiff[cz + 2 : rows, :] = jnp.zeros((rows - cz - 2, 128), F32)
     for ref in (field, zfield, qfield, rfield, pfield):
         ref[...] = jnp.zeros(ref.shape, F32)
     for ref in (vf, wf, syv, dyv, syw, dyw):
@@ -249,28 +274,32 @@
             for t in range(4):
                 ref[t, side % 2] = jnp.zeros(ref.shape[2:], F32)
 
-    def across(a, b):
-        return lax.dot_general(a, b, (((0,), (0,)), ((), ())), precision=HIGH, preferred_element_type=F32)
-
-    def times(a, b):
-        return lax.dot_general(a, b, (((1,), (0,)), ((), ())), precision=HIGH, preferred_element_type=F32)
-
-    def times_t(a, b):
-        return lax.dot_general(a, b, (((1,), (1,)), ((), ())), precision=HIGH, preferred_element_type=F32)
+    for load in loads[:-2]:
+        load.wait()
+    lane_x, lane_y, lane_c = ints[0:8, :], ints[8:16, :], ints[16:24, :]
+    xi_x, xi_y = floats[0:8, :], floats[8:16, :]
+
+    def dot(a, b, dims):
+        return lax.dot_general(a, b, ((dims[:1], dims[1:]), ((), ())), preferred_element_type=F32)
+
+    def spread_in(x):
+        return add_all([dot(part, place[...], (0, 0)) for part in thirds(x)[::-1]])
+
+    def gather_out(select, x):
+        return add_all([dot(select, part, (1, 1)) for part in thirds(x)[::-1]])
 
     for k in range(3):
-        piece = across(rhs[64 * k : 64 * k + 64, :], place[...])
+        piece = spread_in(rhs[64 * k : 64 * k + 64, :])
         first = LEAD + k * rows + 1
         field[first : first + cz, :] = piece
         rfield[first : first + cz, :] = piece
-    node[1 : 1 + cz, :] = across(nodes_in[...].astype(F32) + 1.0, place[...])
+    node[1 : 1 + cz, :] = dot((nodes_in[...].astype(F32) + 1.0).astype(jnp.bfloat16), place[...], (0, 0))
     for i in range(4):
-        lab = labels[i]
-        value = jnp.zeros(lab.shape, F32)
-        for phase in range(moduli.shape[0]):
-            value = jnp.where(lab == phase, moduli[phase], value)
-        stage[4 * i : 4 * i + 4, :] = value
-    blocks = across(stage[...], place_blocks[...])
+        stage[4 * i : 4 * i + 4, :] = labels[i].astype(F32) + 1.0
+    phases = dot(stage[...].astype(jnp.bfloat16), place_blocks[...], (0, 0))
+    blocks = jnp.zeros(phases.shape, F32)
+    for phase in range(moduli.shape[0]):
+        blocks = jnp.where(phases == float(phase + 1), moduli[phase], blocks)
     field[sbase + 1 : sbase + 1 + cz // 2, :] = blocks
 
     bad_lane = (
@@ -284,12 +313,11 @@
     low = jnp.where(gz == 0, 1, 0)
     high = jnp.where(gz == ngz - 1, cz + 1, cz + 2)
 
-    def grid_tile(i, carry):
+    def grid_tile(i):
         r = sub + 8 * i
-        gridm[pl.ds(pl.multiple_of(8 * i, 8), 8), :] = jnp.where(bad_lane | (r < low) | (r >= high), 0.0, 1.0)
-        return carry
-
-    lax.fori_loop(0, tiles, grid_tile, 0)
+        gridm[pl.ds(tile_at(0, i), 8), :] = jnp.where(bad_lane | (r < low) | (r >= high), 0.0, 1.0)
+
+    each_tile(grid_tile)
 
     def halo(which, side, ref_s, ref_r):
         return pltpu.make_async_remote_copy(
@@ -492,7 +520,7 @@
     def moments(ref):
         def one(i, acc):
             r = [ref[pl.ds(base_of(k, i), 8), :] for k in range(3)]
-            own = node[pl.ds(pl.multiple_of(8 * i, 8), 8), :]
+            own = node[pl.ds(tile_at(0, i), 8), :]
             z = xi_z(i)
             parts = r + [xi_y * r[2] - z * r[1], z * r[0] - xi_x * r[2], xi_x * r[1] - xi_y * r[0]]
             out = []
@@ -507,7 +535,7 @@
             rowm[at : at + 1, :] = jnp.sum(acc[at], axis=0, keepdims=True)
 
     def row_to_lanes():
-        return times_t(jnp.ones((8, 128), F32), rowm[...])
+        return gather_out(jnp.ones((8, 128), jnp.bfloat16), rowm[...])
 
     turned = lax.rem((gy * ngz + gz) * MODES, 128)
 
@@ -552,9 +580,9 @@
         return jnp.sum(whole, axis=1, keepdims=True)
 
     def with_coarse(src, dst):
-        def one(i, carry):
-            own = node[pl.ds(pl.multiple_of(8 * i, 8), 8), :]
-            grid = gridm[pl.ds(pl.multiple_of(8 * i, 8), 8), :]
+        def one(i):
+            own = node[pl.ds(tile_at(0, i), 8), :]
+            grid = gridm[pl.ds(tile_at(0, i), 8), :]
             z = xi_z(i)
             modes = [jnp.zeros((8, 128), F32) for _ in range(6)]
             for g in range(NODES):
@@ -571,13 +599,12 @@
             for k in range(3):
                 at = pl.ds(base_of(k, i), 8)
                 dst[at, :] = src[at, :] * grid + add[k]
-            return carry
-
-        lax.fori_loop(0, tiles, one, 0)
+
+        each_tile(one)
 
     def spread(ref):
-        def one(i, carry):
-            s = stiff[pl.ds(pl.multiple_of(8 * i, 8), 8), :]
+        def one(i):
+            s = stiff[pl.ds(tile_at(0, i), 8), :]
             for k in range(3):
                 at = pl.ds(base_of(k, i), 8)
                 v = ref[at, :]
@@ -588,9 +615,8 @@
                     ahead, behind = turn(x, -1), turn(x, 1)
                     sy[at, :] = ahead + behind
                     dy[at, :] = ahead - behind
-            return carry
-
-        lax.fori_loop(0, tiles, one, 0)
+
+        each_tile(one)
 
     def couple(u_ref, sy_ref, dy_ref, i):
         def at(ref, k, dz):
@@ -632,11 +658,11 @@
         ], u
 
     def image_tile(i):
-        here = pl.ds(pl.multiple_of(8 * i, 8), 8)
+        here = pl.ds(tile_at(0, i), 8)
         lv, v = couple(vf, syv, dyv, i)
         lw, _ = couple(wf, syw, dyw, i)
         s = stiff[here, :]
-        d = [dmat[pl.ds(pl.multiple_of(rows * f + 8 * i, 8), 8), :] for f in range(6)]
+        d = [dmat[pl.ds(tile_at(rows * f, i), 8), :] for f in range(6)]
         full = ((0, 3, 4), (3, 1, 5), (4, 5, 2))
         out = []
         for m in range(3):
@@ -645,51 +671,64 @@
         return out, v
 
     def local_solve(ref, out):
-        def first(i, carry):
+        def first(i):
             for k in range(3):
                 at = pl.ds(base_of(k, i), 8)
-                out[at, :] = cdiag[pl.ds(pl.multiple_of(rows * k + 8 * i, 8), 8), :] * ref[at, :]
-            return carry
-
-        lax.fori_loop(0, tiles, first, 0)
+                out[at, :] = cdiag[pl.ds(tile_at(rows * k, i), 8), :] * ref[at, :]
+
+        each_tile(first)
 
         def sweep(n, carry):
             spread(out)
 
-            def one(i, inner):
+            def one(i):
                 image, v = image_tile(i)
                 for k in range(3):
                     at = pl.ds(base_of(k, i), 8)
-                    c = cdiag[pl.ds(pl.multiple_of(rows * k + 8 * i, 8), 8), :]
+                    c = cdiag[pl.ds(tile_at(rows * k, i), 8), :]
                     out[at, :] = v[k] + c * (ref[at, :] - image[k])
-                return inner
-
-            lax.fori_loop(0, tiles, one, 0)
+
+            each_tile(one)
             return carry
 
         lax.fori_loop(0, SWEEPS - 1, sweep, 0)
 
     def setup_stiffness():
-        blocks_all = field[sbase : sbase + srows, :]
-        fine = times(grow[...], blocks_all)
-        flat, both, tilt = fine[0:rows], fine[rows : 2 * rows], fine[2 * rows : 3 * rows]
-        for f in range(7):
-            total_f = None
-            if f < 5:
-                total_f = times(flat, w0[:, 128 * f : 128 * f + 128])
-            if 1 <= f < 5:
-                total_f = total_f + times(both, ws[:, 128 * (f - 1) : 128 * f])
-            if f >= 5:
-                total_f = times(tilt, wd[:, 128 * (f - 5) : 128 * (f - 4)])
-            if f == 0:
-                stiff[...] = total_f
-            else:
-                dmat[rows * (f - 1) : rows * f, :] = total_f
-        r = lax.broadcasted_iota(jnp.int32, (rows, 128), 0)
-        for k in range(3):
-            d = dmat[rows * k : rows * k + rows, :]
-            live = (r < cz + 2) & (d > 0.0)
-            cdiag[rows * k : rows * k + rows, :] = jnp.where(live, RELAX / jnp.where(live, d, 1.0), 0.0)
+        mix_copy.wait()
+        parts = thirds(field[sbase : sbase + srows, :])[::-1]
+        for f in range(0, 11, 2):
+            wide = 128 * min(2, 11 - f)
+            got = add_all([dot(part, mix[:, 128 * f : 128 * f + wide], (1, 0)) for part in parts])
+            for g in range(wide // 128):
+                mixed[srows * (f + g) : srows * (f + g + 1), :] = got[:, 128 * g : 128 * g + 128]
+        count = cz // 2 + 1
+
+        def at(f, shift):
+            return mixed[srows * f + shift : srows * f + shift + count, :]
+
+        for parity in range(2):
+            here = lambda f: at(f, parity)
+            beyond = lambda f: at(f, 1 - parity)
+            s_here = here(0)
+            stiff[pl.ds(parity, count, stride=2), :] = s_here
+            for m in range(6):
+                if m < 4:
+                    value = (here(1 + m) + here(5 + m) + beyond(5 + m)) * (1.0 / 144.0)
+                    if m < 3:
+                        value = value + (0.5 * WHOLE) * s_here
+                else:
+                    tilt = here(5 + m) - beyond(5 + m)
+                    value = (tilt if parity == 1 else -tilt) * (1.0 / 144.0)
+                dmat[pl.ds(rows * m + parity, count, stride=2), :] = value
+
+        def one(i):
+            for k in range(3):
+                part = pl.ds(tile_at(rows * k, i), 8)
+                d = dmat[part, :]
+                live = d > 0.0
+                cdiag[part, :] = jnp.where(live, RELAX / jnp.where(live, d, 1.0), 0.0)
+
+        each_tile(one)
 
     moments(field)
     first_row = turn_by(row_to_lanes(), turned)
@@ -720,7 +759,7 @@
     def image_and_sums(dst, first, second):
         def one(i, acc):
             image, v = image_tile(i)
-            own = node[pl.ds(pl.multiple_of(8 * i, 8), 8), :] > 0.0
+            own = node[pl.ds(tile_at(0, i), 8), :] > 0.0
             acc = list(acc)
             for k in range(3):
                 at = pl.ds(base_of(k, i), 8)
@@ -755,14 +794,13 @@
     with_coarse(pfield, field)
     exchange(field, 3, 2)
 
-    def renew(i, carry):
+    def renew(i):
         for k in range(3):
             at = pl.ds(base_of(k, i), 8)
             field[at, :] = zfield[at, :] - alpha0 * field[at, :]
             rfield[at, :] = rfield[at, :] - alpha0 * qfield[at, :]
-        return carry
-
-    lax.fori_loop(0, tiles, renew, 0)
+
+    each_tile(renew)
     spread(field)
 
     sums = image_and_sums(pfield, rfield, qfield)
@@ -782,8 +820,8 @@
     for k in range(3):
         at = slice(LEAD + k * rows + 1, LEAD + k * rows + 1 + cz)
         z0, z1 = zfield[at, :], field[at, :]
-        sol_out[64 * k : 64 * k + 64, :] = times_t(place[...], alpha0 * z0 + alpha1 * (z1 + beta * z0))
-        res_out[64 * k : 64 * k + 64, :] = times_t(
+        sol_out[64 * k : 64 * k + 64, :] = gather_out(place[...], alpha0 * z0 + alpha1 * (z1 + beta * z0))
+        res_out[64 * k : 64 * k + 64, :] = gather_out(
             place[...], rfield[at, :] - alpha1 * (pfield[at, :] + beta * qfield[at, :])
         )
 
@@ -815,21 +853,29 @@
         ydeep = max(total // 10, 8 * -(-3 * rows // 40))
         xdeep = max(total // 10, 8 * -(-3 * rows // 48))
         vmem = pl.BlockSpec(memory_space=pltpu.VMEM)
+        away = pl.BlockSpec(memory_space=pl.ANY)
         consts = tables(cz)
         sol, res = pl.pallas_call(
             functools.partial(kernel, sizes, cz),
             out_shape=(jax.ShapeDtypeStruct((192, cz), F32),) * 2,
             in_specs=[
-                vmem,
-                vmem,
+                away,
+                away,
                 pl.BlockSpec(memory_space=pltpu.SMEM),
-                vmem,
-                pl.BlockSpec(memory_space=pl.ANY),
+                away,
+                away,
             ]
-            + [vmem] * len(consts),
+            + [away] * len(consts),
             out_specs=(vmem, vmem),
             scratch_shapes=[
                 pltpu.VMEM(coarse_inverse.shape, F32),
+                pltpu.VMEM((192, cz), F32),
+                pltpu.VMEM(phase_labels.shape, jnp.int32),
+                pltpu.VMEM((64, cz), jnp.int32),
+            ]
+            + [pltpu.VMEM(c.shape, c.dtype) for c in consts]
+            + [
+                pltpu.VMEM((11 * srows + 8, 128), F32),
                 tall,
                 tall,
                 tall,
@@ -860,7 +906,7 @@
                 pltpu.VMEM((3, nline, 128), F32),
                 pltpu.VMEM((3, nline, 128), F32),
                 pltpu.VMEM((3, nplane, nline, 128), F32),
-                pltpu.SemaphoreType.DMA,
+                pltpu.SemaphoreType.DMA((9,)),
                 pltpu.SemaphoreType.DMA((4, 6)),
                 pltpu.SemaphoreType.DMA((4, 6)),
                 pltpu.SemaphoreType.DMA((3, nline)),
@@ -869,7 +915,7 @@
                 pltpu.SemaphoreType.DMA((3, nplane)),
             ],
             compiler_params=pltpu.CompilerParams(
-                collective_id=0, has_side_effects=True, vmem_limit_bytes=48 * 1024 * 1024
+                collective_id=0, has_side_effects=True, vmem_limit_bytes=67_000_000
             ),
             name="schwarz_cg",
         )(

time: 120 us -> 96.3 us (0.80)
  Pallas kernels: 107 us -> 92.4 us
  local copies, waits for them, and re-layouts: 12.3 us -> 3.08 us
    pallas_call x1, Pallas kernels: 107 us -> 92.4 us  [body(): pl.pallas_call(functools.partial(kernel, sizes, cz), out_shape=(jax.Shape...]
    unnamed x28 -> x2, local copies, waits for them, and re-layouts: 12.3 us -> 3.08 us
where the time goes in v2:
time: 96.3 us; the launch traced here: 96.1 us
  Pallas kernels  92.4 us (96%)
  local copies, waits for them, and re-layouts  3.08 us (3%)
    pallas_call x1, Pallas kernels, body(): pl.pallas_call(functools.partial(kernel, sizes, cz), out_shape=(jax.Shape...  92.4 us
    unnamed x2, local copies, waits for them, and re-layouts  3.08 us

profile of v2, /device:TPU:1, one launch (start us, length us, event | category | flops | bytes accessed | tf_op | source)
XLA Modules:
  0.0 96.1 jit_solution(15589999831133798248)
XLA Ops:
  0.6 92.4 %schwarz_cg.1 = (f32[192,128]{1,0:T(8,128)}, f32[192,128]{1,0:T(8,128)}) custom-call(f32[192,128]{1,0:T(8,128)} %bitcast.4, s32[4,4,64]{2,1,0:T(4,128)} %labels_hbm.1, f32[8]{0:T(128)} %moduli.1, s32[64,128]{1,0:T(8,128)} %bitcast.7, f32[36,9216]{1,0:T(8,128)} %inverse.1, bf16[64,128]{1,0:T(8,128)(2,1)} %constant.10.clone.place_hbm, ...), custom_call_target="tpu_custom_call" | custom-call | tf_op jit(solution)/shard_map/schwarz_cg/pallas_call | solution.py:858
  93.1 1.5 %copy.14 = f32[3,8,8,128]{3,2,1,0:T(8,128)} copy(f32[3,8,8,128]{3,2,1,0:T(8,128)} %bitcast.6) | data formatting | bytes 196608
  94.6 1.5 %copy.15 = f32[3,8,8,128]{3,2,1,0:T(8,128)} copy(f32[3,8,8,128]{3,2,1,0:T(8,128)} %bitcast.5) | data formatting | bytes 196608

commit v3 on v2

--- a/solution.py
+++ b/solution.py
@@ -19,6 +19,7 @@
 LEAD = 8
 ZH = 2
 NODES = 6
+NEIGHBOURS = [(x, y, z) for x in (-1, 0, 1) for y in (-1, 0, 1) for z in (-1, 0, 1) if (x, y, z) != (0, 0, 0)]
 MODES = 36
 
 
@@ -156,6 +157,11 @@
     yrecv,
     xsend,
     xrecv,
+    csend,
+    crecv,
+    rsend,
+    rrecv,
+    zsum,
     gmsg,
     g1,
     g1c,
@@ -187,17 +193,17 @@
         other = lax.rem(slot2 + step, nplane)
         return (lax.div(other, ngz) * ZH + zhi, gy, lax.rem(other, ngz))
 
-    sides = (
-        (gz > 0, (gx, gy, gz - 1)),
-        (gz < ngz - 1, (gx, gy, gz + 1)),
-        (gy > 0, (gx, gy - 1, gz)),
-        (gy < ngy - 1, (gx, gy + 1, gz)),
-        (gx > 0, (gx - 1, gy, gz)),
-        (gx < ngx - 1, (gx + 1, gy, gz)),
-    )
+    sides = {}
+    for d in NEIGHBOURS:
+        has = None
+        for way, at, count in zip(d, (gx, gy, gz), sizes):
+            if way != 0:
+                one = at > 0 if way < 0 else at < count - 1
+                has = one if has is None else has & one
+        sides[d] = (has, (gx + d[0], gy + d[1], gz + d[2]))
 
     barrier = pltpu.get_barrier_semaphore()
-    for has, device in sides:
+    for has, device in sides.values():
 
         @pl.when(has)
         def _(device=device):
@@ -253,6 +259,42 @@
         along = (sub + (8 * i - 1)).astype(F32)
         return (2.0 * along + 1.0) / cz - 1.0
 
+    def deep(axis, width):
+        if width == 1:
+            return total // 10
+        return 8 * -(-3 * rows // (40 if axis == 1 else 48))
+
+    def edge_deep(width):
+        return 8 * -(-deep(1, width) // 48)
+
+    def inbox(which, d):
+        x, y, z = d
+        width = 1 + which % 2
+        if z != 0:
+            if x == 0:
+                return zrecv.at[which, 3 * (z > 0) + y + 1]
+            at = 6 * (x > 0) + 3 * (z > 0) + y + 1
+            return rrecv.at[which, at : at + 1]
+        if x != 0 and y != 0:
+            return crecv.at[which, 2 * (x > 0) + (y > 0), 0 : edge_deep(width)]
+        if y != 0:
+            return yrecv.at[which, int(y > 0), 0 : deep(1, width)]
+        return xrecv.at[which, int(x > 0), 0 : deep(2, width)]
+
+    def outbox(which, d):
+        x, y, z = d
+        width = 1 + which % 2
+        if z != 0:
+            if x == 0:
+                return zsend.at[which, int(z > 0)]
+            at = 2 * (x > 0) + (z > 0)
+            return rsend.at[which, at, 0:1]
+        if x != 0 and y != 0:
+            return csend.at[which, 2 * (x > 0) + (y > 0), 0 : edge_deep(width)]
+        if y != 0:
+            return ysend.at[which, int(y > 0), 0 : deep(1, width)]
+        return xsend.at[which, int(x > 0), 0 : deep(2, width)]
+
     for f in range(6):
         dmat[rows * f + cz + 2 : rows * (f + 1), :] = jnp.zeros((rows - cz - 2, 128), F32)
     stiff[cz + 2 : rows, :] = jnp.zeros((rows - cz - 2, 128), F32)
@@ -263,16 +305,23 @@
         ref[LEAD + 3 * rows : LEAD + 3 * rows + 8, :] = jnp.zeros((8, 128), F32)
     node[...] = jnp.zeros(node.shape, F32)
     rowm[...] = jnp.zeros(rowm.shape, F32)
-    zsend[...] = jnp.zeros(zsend.shape, F32)
+    for ref in (zsend, ysend):
+        ref[...] = jnp.zeros(ref.shape, F32)
+    tail = deep(1, 1)
+    if tail < yrecv.shape[2]:
+        for t in range(4):
+            for e in range(2):
+                end = deep(1, 1 + t % 2)
+                yrecv[t, e, end:, :] = jnp.zeros((yrecv.shape[2] - end, 128), F32)
     cvec[...] = jnp.zeros(cvec.shape, F32)
     stage[...] = jnp.zeros(stage.shape, F32)
-    for side, (has, _) in enumerate(sides):
-
-        @pl.when(jnp.logical_not(has))
-        def _(side=side):
-            ref = (zrecv, yrecv, xrecv)[side // 2]
+    for d in NEIGHBOURS:
+
+        @pl.when(jnp.logical_not(sides[d][0]))
+        def _(d=d):
             for t in range(4):
-                ref[t, side % 2] = jnp.zeros(ref.shape[2:], F32)
+                ref = inbox(t, d)
+                ref[...] = jnp.zeros(ref.shape, F32)
 
     for load in loads[:-2]:
         load.wait()
@@ -319,43 +368,49 @@
 
     each_tile(grid_tile)
 
-    def halo(which, side, ref_s, ref_r):
+    def number(d):
+        return 9 * (d[0] + 1) + 3 * (d[1] + 1) + d[2] + 1
+
+    def opposite(d):
+        return (-d[0], -d[1], -d[2])
+
+    def halo(which, d):
         return pltpu.make_async_remote_copy(
-            src_ref=ref_s.at[which, side % 2],
-            dst_ref=ref_r.at[which, 1 - side % 2],
-            send_sem=halo_ss.at[which, side],
-            recv_sem=halo_rs.at[which, side + 1 - 2 * (side % 2)],
-            device_id=sides[side][1],
+            src_ref=outbox(which, d),
+            dst_ref=inbox(which, opposite(d)),
+            send_sem=halo_ss.at[which, number(d)],
+            recv_sem=halo_rs.at[which, number(opposite(d))],
+            device_id=sides[d][1],
             device_id_type=MESH,
         )
 
-    def start(which, axis, ref_s, ref_r):
-        for side in (2 * axis, 2 * axis + 1):
-
-            @pl.when(sides[side][0])
-            def _(side=side):
-                halo(which, side, ref_s, ref_r).start()
-
-    def arrive(which, axis, ref_s, ref_r):
-        for side in (2 * axis, 2 * axis + 1):
-
-            @pl.when(sides[side][0])
-            def _(side=side):
+    def send(which, group):
+        for d in group:
+
+            @pl.when(sides[d][0])
+            def _(d=d):
+                halo(which, d).start()
+
+    def arrive(which, group):
+        for d in group:
+
+            @pl.when(sides[d][0])
+            def _(d=d):
                 pltpu.make_async_remote_copy(
-                    src_ref=ref_s.at[which, side % 2],
-                    dst_ref=ref_r.at[which, side % 2],
-                    send_sem=halo_ss.at[which, side],
-                    recv_sem=halo_rs.at[which, side],
-                    device_id=sides[side][1],
+                    src_ref=outbox(which, d),
+                    dst_ref=inbox(which, d),
+                    send_sem=halo_ss.at[which, number(d)],
+                    recv_sem=halo_rs.at[which, number(d)],
+                    device_id=sides[d][1],
                     device_id_type=MESH,
                 ).wait_recv()
 
-    def left(which, axis, ref_s, ref_r):
-        for side in (2 * axis, 2 * axis + 1):
-
-            @pl.when(sides[side][0])
-            def _(side=side):
-                halo(which, side, ref_s, ref_r).wait_send()
+    def left(which):
+        for d in NEIGHBOURS:
+
+            @pl.when(sides[d][0])
+            def _(d=d):
+                halo(which, d).wait_send()
 
     def z_rows(width):
         if width == 1:
@@ -368,98 +423,114 @@
                 out.append((r + cz, r, r, r + cz, 2 * k + layer))
         return out
 
-    def pack_z(ref, which, width):
+    def groups(axis, width):
+        if axis == 1:
+            if width == 1:
+                return 10, [lane_y == k for k in range(10)]
+            return 5, [(lane_y == 2 * k) | (lane_y == 2 * k + 1) for k in range(5)]
+        if width == 1:
+            return 10, [lane_x == k for k in range(10)]
+        return 6, [lane_c == k for k in range(6)]
+
+    def move(axis, width):
+        if axis == 1:
+            if width == 1:
+                return 1, (1, 8), (0, 9), (lane_y == 0, lane_y == 9)
+            return 2, (0, 8), (0, 8), (lane_y < 2, (lane_y == 8) | (lane_y == 9))
+        if width == 1:
+            return STRIDE, (STRIDE, 8 * STRIDE), (0, 9 * STRIDE), (lane_x == 0, lane_x == 9)
+        return 21, (0, 88), (0, 88), (lane < 21, (lane >= 88) & (lane < 109))
+
+    def pack(src, first, dsts, axis, width, chunks, depth):
+        gap, froms, _, _ = move(axis, width)
+        masks = groups(axis, width)[1]
+
+        def one(t, carry):
+            low, high = jnp.zeros((8, 128), F32), jnp.zeros((8, 128), F32)
+            for k in range(chunks):
+                tile = src[pl.ds(pl.multiple_of(first + 8 * (k * depth + t), 8), 8), :]
+                low = jnp.where(masks[k], turn(tile, gap * k - froms[0]), low)
+                high = jnp.where(masks[k], turn(tile, gap * k - froms[1]), high)
+            at = pl.ds(pl.multiple_of(8 * t, 8), 8)
+            dsts[0][at, :] = low
+            dsts[1][at, :] = high
+            return carry
+
+        lax.fori_loop(0, depth, one, 0)
+
+    def unpack(dst, first, srcs, axis, width, chunks, depth):
+        gap, _, tos, ends = move(axis, width)
+
+        def one(t, carry):
+            at = pl.ds(pl.multiple_of(8 * t, 8), 8)
+            low, high = srcs[0][at, :], srcs[1][at, :]
+            for k in range(chunks):
+                part = pl.ds(pl.multiple_of(first + 8 * (k * depth + t), 8), 8)
+                tile = dst[part, :]
+                tile = tile + jnp.where(ends[0], turn(low, tos[0] - gap * k), 0.0)
+                tile = tile + jnp.where(ends[1], turn(high, tos[1] - gap * k), 0.0)
+                dst[part, :] = tile
+            return carry
+
+        lax.fori_loop(0, depth, one, 0)
+
+    def exchange(ref, which, width, between=None):
+        chunks = [None, groups(1, width)[0], groups(2, width)[0]]
+        depth = [None, deep(1, width) // 8, deep(2, width) // 8]
+        edge = edge_deep(width) // 8
+        gap, froms, tos, ends = move(2, width)
+        pack(ref, LEAD, [xsend.at[which, e] for e in range(2)], 2, width, chunks[2], depth[2])
+        send(which, [(-1, 0, 0), (1, 0, 0)])
         for up_from, down_from, _, _, at in z_rows(width):
             zsend[which, 0, at : at + 1, :] = ref[down_from : down_from + 1, :]
             zsend[which, 1, at : at + 1, :] = ref[up_from : up_from + 1, :]
-
-    def unpack_z(ref, which, width):
-        for _, _, low_to, high_to, at in z_rows(width):
-            ref[low_to : low_to + 1, :] += zrecv[which, 0, at : at + 1, :]
-            ref[high_to : high_to + 1, :] += zrecv[which, 1, at : at + 1, :]
-
-    def scheme(axis, width):
-        if width == 1:
-            if axis == 1:
-                return 10, total // 80, lambda k: lane_y == k, lambda k: (k - 1, k - 8), (lane_y == 0, lane_y == 9), lambda k: (-k, 9 - k)
-            return (
-                10,
-                total // 80,
-                lambda k: lane_x == k,
-                lambda k: (STRIDE * (k - 1), STRIDE * (k - 8)),
-                (lane_x == 0, lane_x == 9),
-                lambda k: (-STRIDE * k, STRIDE * (9 - k)),
-            )
-        if axis == 1:
-            return (
-                5,
-                -(-3 * rows // 40),
-                lambda k: (lane_y == 2 * k) | (lane_y == 2 * k + 1),
-                lambda k: (2 * k, 2 * k - 8),
-                (lane_y < 2, (lane_y == 8) | (lane_y == 9)),
-                lambda k: (-2 * k, 8 - 2 * k),
-            )
-        return (
-            6,
-            -(-3 * rows // 48),
-            lambda k: lane_c == k,
-            lambda k: (21 * k, 21 * k - 88),
-            (lane < 21, (lane >= 88) & (lane < 109)),
-            lambda k: (-21 * k, 88 - 21 * k),
-        )
-
-    def pack(ref, which, axis, width, buf):
-        chunks, deep, mask, shift, _, _ = scheme(axis, width)
-        masks = [mask(k) for k in range(chunks)]
-
-        def one(t, carry):
-            down, up = jnp.zeros((8, 128), F32), jnp.zeros((8, 128), F32)
-            for k in range(chunks):
-                tile = ref[pl.ds(pl.multiple_of(LEAD + 8 * (k * deep + t), 8), 8), :]
-                down = jnp.where(masks[k], turn(tile, shift(k)[0]), down)
-                up = jnp.where(masks[k], turn(tile, shift(k)[1]), up)
-            at = pl.ds(pl.multiple_of(8 * t, 8), 8)
-            buf[which, 0, at, :] = down
-            buf[which, 1, at, :] = up
-            return carry
-
-        lax.fori_loop(0, deep, one, 0)
-
-    def unpack(ref, which, axis, width, buf):
-        chunks, deep, _, _, ends, shift = scheme(axis, width)
-
-        def one(t, carry):
-            at = pl.ds(pl.multiple_of(8 * t, 8), 8)
-            from_low, from_high = buf[which, 0, at, :], buf[which, 1, at, :]
-            for k in range(chunks):
-                rows_k = pl.ds(pl.multiple_of(LEAD + 8 * (k * deep + t), 8), 8)
-                tile = ref[rows_k, :]
-                tile = tile + jnp.where(ends[0], turn(from_low, shift(k)[0]), 0.0)
-                tile = tile + jnp.where(ends[1], turn(from_high, shift(k)[1]), 0.0)
-                ref[rows_k, :] = tile
-            return carry
-
-        lax.fori_loop(0, deep, one, 0)
-
-    def cut(ref, axis, width):
-        deep = 8 * scheme(axis, width)[1]
-        return ref.at[:, :, 0:deep, :]
-
-    def exchange(ref, which, width, between=None):
-        pack_z(ref, which, width)
-        start(which, 0, zsend, zrecv)
-        arrive(which, 0, zsend, zrecv)
-        unpack_z(ref, which, width)
-        pack(ref, which, 1, width, ysend)
-        start(which, 1, cut(ysend, 1, width), cut(yrecv, 1, width))
-        arrive(which, 1, cut(ysend, 1, width), cut(yrecv, 1, width))
-        unpack(ref, which, 1, width, yrecv)
-        pack(ref, which, 2, width, xsend)
-        start(which, 2, cut(xsend, 2, width), cut(xrecv, 2, width))
+        layers = 4 if width == 1 else 6
+        mine = [(sub == r) & (lane >= gap * r) & (lane < gap * r + gap) for r in range(layers)]
+        for z in range(2):
+            tile = zsend[which, z]
+            for x in range(2):
+                row = jnp.zeros((8, 128), F32)
+                for r in range(layers):
+                    row = jnp.where(mine[r], turn(tile, gap * r - froms[x]), row)
+                rsend[which, 2 * x + z, 0:1, :] = jnp.sum(row, axis=0, keepdims=True)
+        send(which, [(x, y, z) for x in (-1, 1) for z in (-1, 1) for y in (-1, 0, 1)])
+        pack(ref, LEAD, [ysend.at[which, e] for e in range(2)], 1, width, chunks[1], depth[1])
+        for y in range(2):
+            pack(ysend.at[which, y], 0, [csend.at[which, 2 * x + y] for x in range(2)], 2, width, 6, edge)
+        send(which, [(x, y, 0) for x in (-1, 1) for y in (-1, 1)])
+        send(which, [(0, -1, 0), (0, 1, 0)])
+        send(which, [(0, y, z) for z in (-1, 1) for y in (-1, 0, 1)])
         if between is not None:
             between()
-        arrive(which, 2, cut(xsend, 2, width), cut(xrecv, 2, width))
-        unpack(ref, which, 2, width, xrecv)
+        arrive(which, [(0, y, z) for z in (-1, 1) for y in (-1, 0, 1)])
+        arrive(which, [(0, -1, 0), (0, 1, 0)])
+        arrive(which, [(x, y, z) for x in (-1, 1) for z in (-1, 1) for y in (-1, 0, 1)])
+        yends = move(1, width)[3]
+        for z in range(2):
+            tiles_y = []
+            for y in range(3):
+                tile = zrecv[which, 3 * z + y]
+                for x in range(2):
+                    at = 6 * x + 3 * z + y
+                    row = jnp.broadcast_to(rrecv[which, at : at + 1, :], (8, 128))
+                    for r in range(layers):
+                        here = (sub == r) & ends[x]
+                        tile = tile + jnp.where(here, turn(row, tos[x] - gap * r), 0.0)
+                tiles_y.append(tile)
+            zsum[z] = (
+                tiles_y[1]
+                + jnp.where(yends[0], turn(tiles_y[0], -8), 0.0)
+                + jnp.where(yends[1], turn(tiles_y[2], 8), 0.0)
+            )
+        arrive(which, [(x, y, 0) for x in (-1, 1) for y in (-1, 1)])
+        for y in range(2):
+            unpack(yrecv.at[which, y], 0, [crecv.at[which, 2 * x + y] for x in range(2)], 2, width, 6, edge)
+        unpack(ref, LEAD, [yrecv.at[which, e] for e in range(2)], 1, width, chunks[1], depth[1])
+        arrive(which, [(-1, 0, 0), (1, 0, 0)])
+        unpack(ref, LEAD, [xrecv.at[which, e] for e in range(2)], 2, width, chunks[2], depth[2])
+        for _, _, low_to, high_to, at in z_rows(width):
+            ref[low_to : low_to + 1, :] += zsum[0, at : at + 1, :]
+            ref[high_to : high_to + 1, :] += zsum[1, at : at + 1, :]
 
     def line_copy(which, step):
         return pltpu.make_async_remote_copy(
@@ -733,19 +804,19 @@
     moments(field)
     first_row = turn_by(row_to_lanes(), turned)
     greeters = nline - 1 + nplane - 1
-    for has, _ in sides:
+    for has, _ in sides.values():
         greeters = greeters + jnp.where(has, 1, 0)
     pl.semaphore_wait(barrier, greeters)
 
-    def forward(which):
+    def forward(which, row):
         def run():
+            line_start(which, row)
             line_arrive(which)
             plane_start(which, g1[which])
 
         return run
 
-    line_start(0, first_row)
-    exchange(field, 0, 1, forward(0))
+    exchange(field, 0, 1, forward(0, first_row))
     setup_stiffness()
     local_solve(field, pfield)
     mat_copy.wait()
@@ -781,10 +852,9 @@
     rowm[MODES + 1 : MODES + 2, :] = sums[1]
     second_row = turn_by(row_to_lanes(), turned)
 
-    line_start(1, second_row)
     for k in range(3):
         field[LEAD + rows * k : LEAD + rows * (k + 1), :] = qfield[LEAD + rows * k : LEAD + rows * (k + 1), :]
-    exchange(field, 2, 1, forward(1))
+    exchange(field, 2, 1, forward(1, second_row))
     local_solve(field, pfield)
     plane_arrive(1)
     coarse_solve(1)
@@ -826,10 +896,7 @@
         )
 
     for which in range(4):
-        width = 1 + which % 2
-        left(which, 0, zsend, zrecv)
-        left(which, 1, cut(ysend, 1, width), cut(yrecv, 1, width))
-        left(which, 2, cut(xsend, 2, width), cut(xrecv, 2, width))
+        left(which)
     for which in range(3):
         for step in range(1, nline):
             line_copy(which, step).wait_send()
@@ -851,6 +918,8 @@
         rows, srows, total = plan(cz)
         tall = pltpu.VMEM((LEAD + total, 128), F32)
         ydeep = max(total // 10, 8 * -(-3 * rows // 40))
+        cdeep = 8 * -(-ydeep // 48)
+        ydeep = 6 * cdeep
         xdeep = max(total // 10, 8 * -(-3 * rows // 48))
         vmem = pl.BlockSpec(memory_space=pltpu.VMEM)
         away = pl.BlockSpec(memory_space=pl.ANY)
@@ -897,18 +966,23 @@
                 pltpu.VMEM((40, 128), F32),
                 pltpu.VMEM((16 * sizes[0], 128), F32),
                 pltpu.VMEM((4, 2, 8, 128), F32),
-                pltpu.VMEM((4, 2, 8, 128), F32),
+                pltpu.VMEM((4, 6, 8, 128), F32),
                 pltpu.VMEM((4, 2, ydeep, 128), F32),
                 pltpu.VMEM((4, 2, ydeep, 128), F32),
                 pltpu.VMEM((4, 2, xdeep, 128), F32),
                 pltpu.VMEM((4, 2, xdeep, 128), F32),
+                pltpu.VMEM((4, 4, cdeep, 128), F32),
+                pltpu.VMEM((4, 4, cdeep, 128), F32),
+                pltpu.VMEM((4, 4, 8, 128), F32),
+                pltpu.VMEM((4, 16, 128), F32),
+                pltpu.VMEM((2, 8, 128), F32),
                 pltpu.VMEM((3, 8, 128), F32),
                 pltpu.VMEM((3, nline, 128), F32),
                 pltpu.VMEM((3, nline, 128), F32),
                 pltpu.VMEM((3, nplane, nline, 128), F32),
                 pltpu.SemaphoreType.DMA((9,)),
-                pltpu.SemaphoreType.DMA((4, 6)),
-                pltpu.SemaphoreType.DMA((4, 6)),
+                pltpu.SemaphoreType.DMA((4, 27)),
+                pltpu.SemaphoreType.DMA((4, 27)),
                 pltpu.SemaphoreType.DMA((3, nline)),
                 pltpu.SemaphoreType.DMA((3, nline)),
                 pltpu.SemaphoreType.DMA((3, nplane)),

time: 96.3 us -> 85.4 us (0.89)
  Pallas kernels: 92.4 us -> 81.5 us
    pallas_call x1, Pallas kernels: 92.4 us -> 81.5 us  [body(): pl.pallas_call(functools.partial(kernel, sizes, cz), out_shape=(jax.Shape...]
where the time goes in v3:
time: 85.4 us; the launch traced here: 85.2 us
  Pallas kernels  81.5 us (95%)
  local copies, waits for them, and re-layouts  3.08 us (4%)
    pallas_call x1, Pallas kernels, body(): pl.pallas_call(functools.partial(kernel, sizes, cz), out_shape=(jax.Shape...  81.5 us
    unnamed x2, local copies, waits for them, and re-layouts  3.08 us

profile of v3, /device:TPU:1, one launch (start us, length us, event | category | flops | bytes accessed | tf_op | source)
XLA Modules:
  0.0 85.2 jit_solution(17534238145565210550)
XLA Ops:
  0.6 81.5 %schwarz_cg.1 = (f32[192,128]{1,0:T(8,128)}, f32[192,128]{1,0:T(8,128)}) custom-call(f32[192,128]{1,0:T(8,128)} %bitcast.4, s32[4,4,64]{2,1,0:T(4,128)} %labels_hbm.1, f32[8]{0:T(128)} %moduli.1, s32[64,128]{1,0:T(8,128)} %bitcast.7, f32[36,9216]{1,0:T(8,128)} %inverse.1, bf16[64,128]{1,0:T(8,128)(2,1)} %constant.10.clone.place_hbm, ...), custom_call_target="tpu_custom_call" | custom-call | tf_op jit(solution)/shard_map/schwarz_cg/pallas_call | solution.py:927
  82.1 1.5 %copy.14 = f32[3,8,8,128]{3,2,1,0:T(8,128)} copy(f32[3,8,8,128]{3,2,1,0:T(8,128)} %bitcast.6) | data formatting | bytes 196608
  83.6 1.5 %copy.15 = f32[3,8,8,128]{3,2,1,0:T(8,128)} copy(f32[3,8,8,128]{3,2,1,0:T(8,128)} %bitcast.5) | data formatting | bytes 196608

commit v4 on v3

--- a/solution.py
+++ b/solution.py
@@ -13,6 +13,7 @@
 F32 = jnp.float32
 
 RELAX = 0.6
+UNROLL = 4
 SWEEPS = 4
 SIDE = 8
 STRIDE = 11
@@ -71,10 +72,11 @@
                         mix[src, 128 * (5 + at) + out] += 72.0 * coef(m, k, (a, b, 1))
     mix = np.round(mix)
     lane = np.arange(128)
-    ints = np.zeros((24, 128), np.int32)
+    ints = np.zeros((32, 128), np.int32)
     ints[0:8] = np.where(lane < 110, lane // STRIDE, 99)
     ints[8:16] = np.where(lane < 110, lane % STRIDE, 99)
     ints[16:24] = np.where(lane < 126, lane // 21, 99)
+    ints[24:32] = np.where(lane < 126, lane % 21 % STRIDE, 99)
     floats = np.zeros((16, 128), np.float32)
     floats[0:8] = (2.0 * (lane // STRIDE - 1) + 1.0) / SIDE - 1.0
     floats[8:16] = (2.0 * (lane % STRIDE - 1) + 1.0) / SIDE - 1.0
@@ -136,12 +138,8 @@
     qfield,
     rfield,
     pfield,
-    vf,
-    wf,
-    syv,
-    dyv,
-    syw,
-    dyw,
+    set_a,
+    set_b,
     dmat,
     stiff,
     cdiag,
@@ -162,6 +160,7 @@
     rsend,
     rrecv,
     zsum,
+    outs,
     gmsg,
     g1,
     g1c,
@@ -202,18 +201,6 @@
                 has = one if has is None else has & one
         sides[d] = (has, (gx + d[0], gy + d[1], gz + d[2]))
 
-    barrier = pltpu.get_barrier_semaphore()
-    for has, device in sides.values():
-
-        @pl.when(has)
-        def _(device=device):
-            pl.semaphore_signal(barrier, inc=1, device_id=device, device_id_type=MESH)
-
-    for step in range(1, nline):
-        pl.semaphore_signal(barrier, inc=1, device_id=line_peer(step), device_id_type=MESH)
-    for step in range(1, nplane):
-        pl.semaphore_signal(barrier, inc=1, device_id=plane_peer(step), device_id_type=MESH)
-
     loads = [
         pltpu.make_async_copy(src, dst, load_sem.at[at])
         for at, (src, dst) in enumerate(
@@ -234,6 +221,19 @@
         load.start()
     mat_copy, mix_copy = loads[-1], loads[-2]
 
+    barrier = pltpu.get_barrier_semaphore()
+    for has, device in [sides[d] for d in sorted(NEIGHBOURS, key=lambda d: -abs(d[0]))]:
+
+        @pl.when(has)
+        def _(device=device):
+            pl.semaphore_signal(barrier, inc=1, device_id=device, device_id_type=MESH)
+
+    for step in range(1, nline):
+        pl.semaphore_signal(barrier, inc=1, device_id=line_peer(step), device_id_type=MESH)
+    for step in range(1, nplane):
+        pl.semaphore_signal(barrier, inc=1, device_id=plane_peer(step), device_id_type=MESH)
+
+
     lane = lax.broadcasted_iota(jnp.int32, (8, 128), 1)
     sub = lax.broadcasted_iota(jnp.int32, (8, 128), 0)
 
@@ -264,8 +264,11 @@
             return total // 10
         return 8 * -(-3 * rows // (40 if axis == 1 else 48))
 
+    def edge_chunks(width):
+        return 6 if width == 1 else 5
+
     def edge_deep(width):
-        return 8 * -(-deep(1, width) // 48)
+        return 8 * -(-deep(2, width) // (8 * edge_chunks(width)))
 
     def inbox(which, d):
         x, y, z = d
@@ -298,21 +301,20 @@
     for f in range(6):
         dmat[rows * f + cz + 2 : rows * (f + 1), :] = jnp.zeros((rows - cz - 2, 128), F32)
     stiff[cz + 2 : rows, :] = jnp.zeros((rows - cz - 2, 128), F32)
-    for ref in (field, zfield, qfield, rfield, pfield):
+    for ref in (field, rfield):
         ref[...] = jnp.zeros(ref.shape, F32)
-    for ref in (vf, wf, syv, dyv, syw, dyw):
+    zfield[sbase:, :] = jnp.zeros((LEAD + total - sbase, 128), F32)
+    for ref in set_a + set_b:
         ref[0:LEAD, :] = jnp.zeros((LEAD, 128), F32)
         ref[LEAD + 3 * rows : LEAD + 3 * rows + 8, :] = jnp.zeros((8, 128), F32)
     node[...] = jnp.zeros(node.shape, F32)
     rowm[...] = jnp.zeros(rowm.shape, F32)
-    for ref in (zsend, ysend):
+    for ref in (zsend, xsend):
         ref[...] = jnp.zeros(ref.shape, F32)
-    tail = deep(1, 1)
-    if tail < yrecv.shape[2]:
-        for t in range(4):
-            for e in range(2):
-                end = deep(1, 1 + t % 2)
-                yrecv[t, e, end:, :] = jnp.zeros((yrecv.shape[2] - end, 128), F32)
+    for t in range(4):
+        for e in range(2):
+            end = deep(2, 1 + t % 2)
+            xrecv[t, e, end:, :] = jnp.zeros((xrecv.shape[2] - end, 128), F32)
     cvec[...] = jnp.zeros(cvec.shape, F32)
     stage[...] = jnp.zeros(stage.shape, F32)
     for d in NEIGHBOURS:
@@ -326,6 +328,7 @@
     for load in loads[:-2]:
         load.wait()
     lane_x, lane_y, lane_c = ints[0:8, :], ints[8:16, :], ints[16:24, :]
+    lane_e = ints[24:32, :]
     xi_x, xi_y = floats[0:8, :], floats[8:16, :]
 
     def dot(a, b, dims):
@@ -423,27 +426,29 @@
                 out.append((r + cz, r, r, r + cz, 2 * k + layer))
         return out
 
-    def groups(axis, width):
+    def groups(axis, width, along=None):
         if axis == 1:
+            along = lane_y if along is None else along
             if width == 1:
-                return 10, [lane_y == k for k in range(10)]
-            return 5, [(lane_y == 2 * k) | (lane_y == 2 * k + 1) for k in range(5)]
+                return 10, [along == k for k in range(10)]
+            return 5, [(along == 2 * k) | (along == 2 * k + 1) for k in range(5)]
         if width == 1:
             return 10, [lane_x == k for k in range(10)]
         return 6, [lane_c == k for k in range(6)]
 
-    def move(axis, width):
+    def move(axis, width, along=None):
         if axis == 1:
+            along = lane_y if along is None else along
             if width == 1:
-                return 1, (1, 8), (0, 9), (lane_y == 0, lane_y == 9)
-            return 2, (0, 8), (0, 8), (lane_y < 2, (lane_y == 8) | (lane_y == 9))
+                return 1, (1, 8), (0, 9), (along == 0, along == 9)
+            return 2, (0, 8), (0, 8), (along < 2, (along == 8) | (along == 9))
         if width == 1:
             return STRIDE, (STRIDE, 8 * STRIDE), (0, 9 * STRIDE), (lane_x == 0, lane_x == 9)
         return 21, (0, 88), (0, 88), (lane < 21, (lane >= 88) & (lane < 109))
 
-    def pack(src, first, dsts, axis, width, chunks, depth):
+    def pack(src, first, dsts, axis, width, chunks, depth, along=None):
         gap, froms, _, _ = move(axis, width)
-        masks = groups(axis, width)[1]
+        masks = groups(axis, width, along)[1]
 
         def one(t, carry):
             low, high = jnp.zeros((8, 128), F32), jnp.zeros((8, 128), F32)
@@ -458,8 +463,8 @@
 
         lax.fori_loop(0, depth, one, 0)
 
-    def unpack(dst, first, srcs, axis, width, chunks, depth):
-        gap, _, tos, ends = move(axis, width)
+    def unpack(dst, first, srcs, axis, width, chunks, depth, along=None):
+        gap, _, tos, ends = move(axis, width, along)
 
         def one(t, carry):
             at = pl.ds(pl.multiple_of(8 * t, 8), 8)
@@ -474,17 +479,34 @@
 
         lax.fori_loop(0, depth, one, 0)
 
-    def exchange(ref, which, width, between=None):
+    far_rows = [(x, y, z) for x in (-1, 1) for z in (-1, 1) for y in (-1, 0, 1)]
+    near_layers = [(0, y, z) for z in (-1, 1) for y in (-1, 0, 1)]
+    edges = [(x, y, 0) for x in (-1, 1) for y in (-1, 1)]
+
+    def exchange(ref, which, width, early=None, late=None):
         chunks = [None, groups(1, width)[0], groups(2, width)[0]]
         depth = [None, deep(1, width) // 8, deep(2, width) // 8]
-        edge = edge_deep(width) // 8
+        edge, edge_parts = edge_deep(width) // 8, edge_chunks(width)
+        along = lane_y if width == 1 else lane_e
         gap, froms, tos, ends = move(2, width)
+        layers = 4 if width == 1 else 6
         pack(ref, LEAD, [xsend.at[which, e] for e in range(2)], 2, width, chunks[2], depth[2])
         send(which, [(-1, 0, 0), (1, 0, 0)])
+        for x in range(2):
+            pack(
+                xsend.at[which, x],
+                0,
+                [csend.at[which, 2 * x + y] for y in range(2)],
+                1,
+                width,
+                edge_parts,
+                edge,
+                along,
+            )
+        send(which, edges)
         for up_from, down_from, _, _, at in z_rows(width):
             zsend[which, 0, at : at + 1, :] = ref[down_from : down_from + 1, :]
             zsend[which, 1, at : at + 1, :] = ref[up_from : up_from + 1, :]
-        layers = 4 if width == 1 else 6
         mine = [(sub == r) & (lane >= gap * r) & (lane < gap * r + gap) for r in range(layers)]
         for z in range(2):
             tile = zsend[which, z]
@@ -493,18 +515,18 @@
                 for r in range(layers):
                     row = jnp.where(mine[r], turn(tile, gap * r - froms[x]), row)
                 rsend[which, 2 * x + z, 0:1, :] = jnp.sum(row, axis=0, keepdims=True)
-        send(which, [(x, y, z) for x in (-1, 1) for z in (-1, 1) for y in (-1, 0, 1)])
+        send(which, far_rows)
         pack(ref, LEAD, [ysend.at[which, e] for e in range(2)], 1, width, chunks[1], depth[1])
-        for y in range(2):
-            pack(ysend.at[which, y], 0, [csend.at[which, 2 * x + y] for x in range(2)], 2, width, 6, edge)
-        send(which, [(x, y, 0) for x in (-1, 1) for y in (-1, 1)])
         send(which, [(0, -1, 0), (0, 1, 0)])
-        send(which, [(0, y, z) for z in (-1, 1) for y in (-1, 0, 1)])
-        if between is not None:
-            between()
-        arrive(which, [(0, y, z) for z in (-1, 1) for y in (-1, 0, 1)])
+        send(which, near_layers)
+        if early is not None:
+            early()
         arrive(which, [(0, -1, 0), (0, 1, 0)])
-        arrive(which, [(x, y, z) for x in (-1, 1) for z in (-1, 1) for y in (-1, 0, 1)])
+        unpack(ref, LEAD, [yrecv.at[which, e] for e in range(2)], 1, width, chunks[1], depth[1])
+        if late is not None:
+            late()
+        arrive(which, near_layers)
+        arrive(which, far_rows)
         yends = move(1, width)[3]
         for z in range(2):
             tiles_y = []
@@ -522,15 +544,23 @@
                 + jnp.where(yends[0], turn(tiles_y[0], -8), 0.0)
                 + jnp.where(yends[1], turn(tiles_y[2], 8), 0.0)
             )
-        arrive(which, [(x, y, 0) for x in (-1, 1) for y in (-1, 1)])
-        for y in range(2):
-            unpack(yrecv.at[which, y], 0, [crecv.at[which, 2 * x + y] for x in range(2)], 2, width, 6, edge)
-        unpack(ref, LEAD, [yrecv.at[which, e] for e in range(2)], 1, width, chunks[1], depth[1])
-        arrive(which, [(-1, 0, 0), (1, 0, 0)])
-        unpack(ref, LEAD, [xrecv.at[which, e] for e in range(2)], 2, width, chunks[2], depth[2])
         for _, _, low_to, high_to, at in z_rows(width):
             ref[low_to : low_to + 1, :] += zsum[0, at : at + 1, :]
             ref[high_to : high_to + 1, :] += zsum[1, at : at + 1, :]
+        arrive(which, [(-1, 0, 0), (1, 0, 0)])
+        arrive(which, edges)
+        for x in range(2):
+            unpack(
+                xrecv.at[which, x],
+                0,
+                [crecv.at[which, 2 * x + y] for y in range(2)],
+                1,
+                width,
+                edge_parts,
+                edge,
+                along,
+            )
+        unpack(ref, LEAD, [xrecv.at[which, e] for e in range(2)], 2, width, chunks[2], depth[2])
 
     def line_copy(which, step):
         return pltpu.make_async_remote_copy(
@@ -560,10 +590,13 @@
                 device_id_type=MESH,
             ).wait_recv()
 
+    def plane_rows(which):
+        return nline if which < 2 else 8
+
     def plane_copy(which, step):
         return pltpu.make_async_remote_copy(
-            src_ref=g1c.at[which],
-            dst_ref=g2.at[which, slot2],
+            src_ref=g1c.at[which, 0 : plane_rows(which)],
+            dst_ref=g2.at[which, slot2, 0 : plane_rows(which)],
             send_sem=g2_ss.at[which, step],
             recv_sem=g2_rs.at[which, slot2],
             device_id=plane_peer(step),
@@ -580,8 +613,8 @@
         for step in range(1, nplane):
             other = lax.rem(slot2 + step, nplane)
             pltpu.make_async_remote_copy(
-                src_ref=g1c.at[which],
-                dst_ref=g2.at[which, other],
+                src_ref=g1c.at[which, 0 : plane_rows(which)],
+                dst_ref=g2.at[which, other, 0 : plane_rows(which)],
                 send_sem=g2_ss.at[which, step],
                 recv_sem=g2_rs.at[which, other],
                 device_id=plane_peer(step),
@@ -673,21 +706,22 @@
 
         each_tile(one)
 
+    def spread_tile(i, values, bufs):
+        vf, wf, syv, dyv, syw, dyw = bufs
+        s = stiff[pl.ds(tile_at(0, i), 8), :]
+        for k in range(3):
+            at = pl.ds(base_of(k, i), 8)
+            v = values[k]
+            w = s * v
+            vf[at, :] = v
+            wf[at, :] = w
+            for x, sy, dy in ((v, syv, dyv), (w, syw, dyw)):
+                ahead, behind = turn(x, -1), turn(x, 1)
+                sy[at, :] = ahead + behind
+                dy[at, :] = ahead - behind
+
     def spread(ref):
-        def one(i):
-            s = stiff[pl.ds(tile_at(0, i), 8), :]
-            for k in range(3):
-                at = pl.ds(base_of(k, i), 8)
-                v = ref[at, :]
-                w = s * v
-                vf[at, :] = v
-                wf[at, :] = w
-                for x, sy, dy in ((v, syv, dyv), (w, syw, dyw)):
-                    ahead, behind = turn(x, -1), turn(x, 1)
-                    sy[at, :] = ahead + behind
-                    dy[at, :] = ahead - behind
-
-        each_tile(one)
+        each_tile(lambda i: spread_tile(i, [ref[pl.ds(base_of(k, i), 8), :] for k in range(3)], set_a))
 
     def couple(u_ref, sy_ref, dy_ref, i):
         def at(ref, k, dz):
@@ -728,7 +762,8 @@
             still[k] + (turn(even[k] + odd[k], -STRIDE) + turn(even[k] - odd[k], STRIDE)) for k in range(3)
         ], u
 
-    def image_tile(i):
+    def image_tile(i, bufs):
+        vf, wf, syv, dyv, syw, dyw = bufs
         here = pl.ds(tile_at(0, i), 8)
         lv, v = couple(vf, syv, dyv, i)
         lw, _ = couple(wf, syw, dyw, i)
@@ -743,26 +778,29 @@
 
     def local_solve(ref, out):
         def first(i):
-            for k in range(3):
-                at = pl.ds(base_of(k, i), 8)
-                out[at, :] = cdiag[pl.ds(tile_at(rows * k, i), 8), :] * ref[at, :]
+            spread_tile(
+                i,
+                [cdiag[pl.ds(tile_at(rows * k, i), 8), :] * ref[pl.ds(base_of(k, i), 8), :] for k in range(3)],
+                set_a,
+            )
 
         each_tile(first)
-
-        def sweep(n, carry):
-            spread(out)
-
-            def one(i):
-                image, v = image_tile(i)
+        bufs = [set_a, set_b]
+        for sweep in range(SWEEPS - 1):
+
+            def one(i, sweep=sweep):
+                image, v = image_tile(i, bufs[sweep % 2])
+                new = []
                 for k in range(3):
-                    at = pl.ds(base_of(k, i), 8)
                     c = cdiag[pl.ds(tile_at(rows * k, i), 8), :]
-                    out[at, :] = v[k] + c * (ref[at, :] - image[k])
-
-            each_tile(one)
-            return carry
-
-        lax.fori_loop(0, SWEEPS - 1, sweep, 0)
+                    new.append(v[k] + c * (ref[pl.ds(base_of(k, i), 8), :] - image[k]))
+                if sweep < SWEEPS - 2:
+                    spread_tile(i, new, bufs[(sweep + 1) % 2])
+                else:
+                    for k in range(3):
+                        out[pl.ds(base_of(k, i), 8), :] = new[k]
+
+            each_tile(one, UNROLL)
 
     def setup_stiffness():
         mix_copy.wait()
@@ -801,22 +839,20 @@
 
         each_tile(one)
 
-    moments(field)
-    first_row = turn_by(row_to_lanes(), turned)
+    def first_row():
+        moments(field)
+        return turn_by(row_to_lanes(), turned)
+
     greeters = nline - 1 + nplane - 1
     for has, _ in sides.values():
         greeters = greeters + jnp.where(has, 1, 0)
     pl.semaphore_wait(barrier, greeters)
 
-    def forward(which, row):
-        def run():
-            line_start(which, row)
-            line_arrive(which)
-            plane_start(which, g1[which])
-
-        return run
-
-    exchange(field, 0, 1, forward(0, first_row))
+    def forward(which):
+        line_arrive(which)
+        plane_start(which, g1[which])
+
+    exchange(field, 0, 1, lambda: line_start(0, first_row()), lambda: forward(0))
     setup_stiffness()
     local_solve(field, pfield)
     mat_copy.wait()
@@ -827,15 +863,16 @@
 
     spread(zfield)
 
-    def image_and_sums(dst, first, second):
+    def image_and_sums(dsts, first, second):
         def one(i, acc):
-            image, v = image_tile(i)
+            image, v = image_tile(i, set_a)
             own = node[pl.ds(tile_at(0, i), 8), :] > 0.0
             acc = list(acc)
             for k in range(3):
                 at = pl.ds(base_of(k, i), 8)
                 mine = jnp.where(own, image[k], 0.0)
-                dst[at, :] = mine
+                for dst in dsts:
+                    dst[at, :] = mine
                 acc[0] = acc[0] + first[at, :] * v[k]
                 acc[1] = acc[1] + v[k] * mine
                 if second is not None:
@@ -846,15 +883,14 @@
         acc = lax.fori_loop(0, tiles, one, tuple(jnp.zeros((8, 128), F32) for _ in range(count)))
         return [jnp.sum(a, axis=0, keepdims=True) for a in acc]
 
-    sums = image_and_sums(qfield, rfield, None)
-    moments(qfield)
-    rowm[MODES : MODES + 1, :] = sums[0]
-    rowm[MODES + 1 : MODES + 2, :] = sums[1]
-    second_row = turn_by(row_to_lanes(), turned)
-
-    for k in range(3):
-        field[LEAD + rows * k : LEAD + rows * (k + 1), :] = qfield[LEAD + rows * k : LEAD + rows * (k + 1), :]
-    exchange(field, 2, 1, forward(1, second_row))
+    sums = image_and_sums((qfield, field), rfield, None)
+    def second_row():
+        moments(qfield)
+        rowm[MODES : MODES + 1, :] = sums[0]
+        rowm[MODES + 1 : MODES + 2, :] = sums[1]
+        return turn_by(row_to_lanes(), turned)
+
+    exchange(field, 2, 1, lambda: line_start(1, second_row()), lambda: forward(1))
     local_solve(field, pfield)
     plane_arrive(1)
     coarse_solve(1)
@@ -873,27 +909,29 @@
     each_tile(renew)
     spread(field)
 
-    sums = image_and_sums(pfield, rfield, qfield)
+    sums = image_and_sums((pfield,), rfield, qfield)
     rowm[0:MODES, :] = jnp.zeros((MODES, 128), F32)
     for at in range(3):
         rowm[MODES + at : MODES + at + 1, :] = sums[at]
-    line_start(2, turn_by(row_to_lanes(), turned))
+    line_start(2, row_to_lanes())
+    for at, ref in enumerate((zfield, field, rfield, pfield, qfield)):
+        for k in range(3):
+            first = LEAD + k * rows + 1
+            outs[192 * at + 64 * k : 192 * at + 64 * k + 64, :] = gather_out(place[...], ref[first : first + cz, :])
     line_arrive(2)
-    plane_start(2, g1[2])
+    plane_start(2, jnp.broadcast_to(jnp.sum(g1[2], axis=0, keepdims=True), (nline, 128)))
     plane_arrive(2)
-    rho1 = lane_sum(2, MODES)
-    zaz = lane_sum(2, MODES + 1)
-    zq = lane_sum(2, MODES + 2)
+    last = add_all([g2[2, p, 0:8, :] for p in range(nplane)])[0:1, :]
+    rho1, zaz, zq = [
+        jnp.sum(jnp.where(lane[0:1, :] == MODES + at, last, 0.0), axis=1, keepdims=True) for at in range(3)
+    ]
     beta = rho1 / rho0
     alpha1 = rho1 / (zaz + 2.0 * beta * zq + beta * beta * curve0)
 
-    for k in range(3):
-        at = slice(LEAD + k * rows + 1, LEAD + k * rows + 1 + cz)
-        z0, z1 = zfield[at, :], field[at, :]
-        sol_out[64 * k : 64 * k + 64, :] = gather_out(place[...], alpha0 * z0 + alpha1 * (z1 + beta * z0))
-        res_out[64 * k : 64 * k + 64, :] = gather_out(
-            place[...], rfield[at, :] - alpha1 * (pfield[at, :] + beta * qfield[at, :])
-        )
+    for i in range(24):
+        z0, z1, r1, q1, q0 = [outs[192 * at + 8 * i : 192 * at + 8 * i + 8, :] for at in range(5)]
+        sol_out[8 * i : 8 * i + 8, :] = alpha0 * z0 + alpha1 * (z1 + beta * z0)
+        res_out[8 * i : 8 * i + 8, :] = r1 - alpha1 * (q1 + beta * q0)
 
     for which in range(4):
         left(which)
@@ -918,9 +956,9 @@
         rows, srows, total = plan(cz)
         tall = pltpu.VMEM((LEAD + total, 128), F32)
         ydeep = max(total // 10, 8 * -(-3 * rows // 40))
-        cdeep = 8 * -(-ydeep // 48)
-        ydeep = 6 * cdeep
+        cdeep = 16
         xdeep = max(total // 10, 8 * -(-3 * rows // 48))
+        xdeep = max(xdeep, 5 * cdeep)
         vmem = pl.BlockSpec(memory_space=pltpu.VMEM)
         away = pl.BlockSpec(memory_space=pl.ANY)
         consts = tables(cz)
@@ -950,12 +988,8 @@
                 tall,
                 tall,
                 tall,
-                tall,
-                tall,
-                tall,
-                tall,
-                tall,
-                tall,
+                (tall,) * 6,
+                (tall,) * 6,
                 pltpu.VMEM((6 * rows, 128), F32),
                 pltpu.VMEM((rows, 128), F32),
                 pltpu.VMEM((3 * rows, 128), F32),
@@ -976,6 +1010,7 @@
                 pltpu.VMEM((4, 4, 8, 128), F32),
                 pltpu.VMEM((4, 16, 128), F32),
                 pltpu.VMEM((2, 8, 128), F32),
+                pltpu.VMEM((5 * 192, cz), F32),
                 pltpu.VMEM((3, 8, 128), F32),
                 pltpu.VMEM((3, nline, 128), F32),
                 pltpu.VMEM((3, nline, 128), F32),

time: 85.4 us -> 81.7 us (0.957)
  Pallas kernels: 81.5 us -> 77.8 us
    pallas_call x1, Pallas kernels: 81.5 us -> 77.8 us  [body(): pl.pallas_call(functools.partial(kernel, sizes, cz), out_shape=(jax.Shape...]
where the time goes in v4:
time: 81.7 us; the launch traced here: 81.5 us
  Pallas kernels  77.8 us (95%)
  local copies, waits for them, and re-layouts  3.08 us (4%)
    pallas_call x1, Pallas kernels, body(): pl.pallas_call(functools.partial(kernel, sizes, cz), out_shape=(jax.Shape...  77.8 us
    unnamed x2, local copies, waits for them, and re-layouts  3.08 us

profile of v4, /device:TPU:1, one launch (start us, length us, event | category | flops | bytes accessed | tf_op | source)
XLA Modules:
  0.0 81.5 jit_solution(3625582209379108413)
XLA Ops:
  0.6 77.8 %schwarz_cg.1 = (f32[192,128]{1,0:T(8,128)}, f32[192,128]{1,0:T(8,128)}) custom-call(f32[192,128]{1,0:T(8,128)} %bitcast.4, s32[4,4,64]{2,1,0:T(4,128)} %labels_hbm.1, f32[8]{0:T(128)} %moduli.1, s32[64,128]{1,0:T(8,128)} %bitcast.7, f32[36,9216]{1,0:T(8,128)} %inverse.1, bf16[64,128]{1,0:T(8,128)(2,1)} %constant.10.clone.place_hbm, ...), custom_call_target="tpu_custom_call" | custom-call | tf_op jit(solution)/shard_map/schwarz_cg/pallas_call | solution.py:965
  78.4 1.5 %copy.14 = f32[3,8,8,128]{3,2,1,0:T(8,128)} copy(f32[3,8,8,128]{3,2,1,0:T(8,128)} %bitcast.6) | data formatting | bytes 196608
  80.0 1.5 %copy.15 = f32[3,8,8,128]{3,2,1,0:T(8,128)} copy(f32[3,8,8,128]{3,2,1,0:T(8,128)} %bitcast.5) | data formatting | bytes 196608

commit v5 on v4

--- a/solution.py
+++ b/solution.py
@@ -243,6 +243,19 @@
     def tile_at(first, i):
         return first + 8 * i if isinstance(i, int) else pl.multiple_of(first + 8 * i, 8)
 
+    def repeat(count, one, unroll):
+        whole = count // unroll if count > 2 * unroll else 0
+
+        def some(n, carry):
+            for j in range(unroll):
+                one(n * unroll + j)
+            return carry
+
+        if whole:
+            lax.fori_loop(0, whole, some, 0)
+        for i in range(whole * unroll, count):
+            one(i)
+
     def each_tile(one, unroll=4):
         whole = tiles // unroll
 
@@ -450,34 +463,32 @@
         gap, froms, _, _ = move(axis, width)
         masks = groups(axis, width, along)[1]
 
-        def one(t, carry):
+        def one(t):
             low, high = jnp.zeros((8, 128), F32), jnp.zeros((8, 128), F32)
             for k in range(chunks):
-                tile = src[pl.ds(pl.multiple_of(first + 8 * (k * depth + t), 8), 8), :]
+                tile = src[pl.ds(tile_at(first + 8 * k * depth, t), 8), :]
                 low = jnp.where(masks[k], turn(tile, gap * k - froms[0]), low)
                 high = jnp.where(masks[k], turn(tile, gap * k - froms[1]), high)
-            at = pl.ds(pl.multiple_of(8 * t, 8), 8)
+            at = pl.ds(tile_at(0, t), 8)
             dsts[0][at, :] = low
             dsts[1][at, :] = high
-            return carry
-
-        lax.fori_loop(0, depth, one, 0)
+
+        repeat(depth, one, 3)
 
     def unpack(dst, first, srcs, axis, width, chunks, depth, along=None):
         gap, _, tos, ends = move(axis, width, along)
 
-        def one(t, carry):
-            at = pl.ds(pl.multiple_of(8 * t, 8), 8)
+        def one(t):
+            at = pl.ds(tile_at(0, t), 8)
             low, high = srcs[0][at, :], srcs[1][at, :]
             for k in range(chunks):
-                part = pl.ds(pl.multiple_of(first + 8 * (k * depth + t), 8), 8)
+                part = pl.ds(tile_at(first + 8 * k * depth, t), 8)
                 tile = dst[part, :]
                 tile = tile + jnp.where(ends[0], turn(low, tos[0] - gap * k), 0.0)
                 tile = tile + jnp.where(ends[1], turn(high, tos[1] - gap * k), 0.0)
                 dst[part, :] = tile
-            return carry
-
-        lax.fori_loop(0, depth, one, 0)
+
+        repeat(depth, one, 3)
 
     far_rows = [(x, y, z) for x in (-1, 1) for z in (-1, 1) for y in (-1, 0, 1)]
     near_layers = [(0, y, z) for z in (-1, 1) for y in (-1, 0, 1)]
@@ -880,7 +891,10 @@
             return tuple(acc)
 
         count = 2 if second is None else 3
-        acc = lax.fori_loop(0, tiles, one, tuple(jnp.zeros((8, 128), F32) for _ in range(count)))
+        acc = tuple(jnp.zeros((8, 128), F32) for _ in range(count))
+        acc = lax.fori_loop(0, tiles // 2, lambda n, acc: one(2 * n + 1, one(2 * n, acc)), acc)
+        for i in range(tiles // 2 * 2, tiles):
+            acc = one(i, acc)
         return [jnp.sum(a, axis=0, keepdims=True) for a in acc]
 
     sums = image_and_sums((qfield, field), rfield, None)

time: 81.7 us -> 77.2 us (0.945)
  Pallas kernels: 77.8 us -> 73.3 us
    pallas_call x1, Pallas kernels: 77.8 us -> 73.3 us  [body(): pl.pallas_call(functools.partial(kernel, sizes, cz), out_shape=(jax.Shape...]
where the time goes in v5:
time: 77.2 us; the launch traced here: 77 us
  Pallas kernels  73.3 us (95%)
  local copies, waits for them, and re-layouts  3.08 us (4%)
    pallas_call x1, Pallas kernels, body(): pl.pallas_call(functools.partial(kernel, sizes, cz), out_shape=(jax.Shape...  73.3 us
    unnamed x2, local copies, waits for them, and re-layouts  3.08 us

profile of v5, /device:TPU:1, one launch (start us, length us, event | category | flops | bytes accessed | tf_op | source)
XLA Modules:
  0.0 77.0 jit_solution(4438787933360854906)
XLA Ops:
  0.6 73.3 %schwarz_cg.1 = (f32[192,128]{1,0:T(8,128)}, f32[192,128]{1,0:T(8,128)}) custom-call(f32[192,128]{1,0:T(8,128)} %bitcast.4, s32[4,4,64]{2,1,0:T(4,128)} %labels_hbm.1, f32[8]{0:T(128)} %moduli.1, s32[64,128]{1,0:T(8,128)} %bitcast.7, f32[36,9216]{1,0:T(8,128)} %inverse.1, bf16[64,128]{1,0:T(8,128)(2,1)} %constant.10.clone.place_hbm, ...), custom_call_target="tpu_custom_call" | custom-call | tf_op jit(solution)/shard_map/schwarz_cg/pallas_call | solution.py:979
  74.0 1.5 %copy.14 = f32[3,8,8,128]{3,2,1,0:T(8,128)} copy(f32[3,8,8,128]{3,2,1,0:T(8,128)} %bitcast.6) | data formatting | bytes 196608
  75.5 1.5 %copy.15 = f32[3,8,8,128]{3,2,1,0:T(8,128)} copy(f32[3,8,8,128]{3,2,1,0:T(8,128)} %bitcast.5) | data formatting | bytes 196608

commit v6 on v5

--- a/solution.py
+++ b/solution.py
@@ -473,7 +473,7 @@
             dsts[0][at, :] = low
             dsts[1][at, :] = high
 
-        repeat(depth, one, 3)
+        repeat(depth, one, 6)
 
     def unpack(dst, first, srcs, axis, width, chunks, depth, along=None):
         gap, _, tos, ends = move(axis, width, along)
@@ -488,7 +488,7 @@
                 tile = tile + jnp.where(ends[1], turn(high, tos[1] - gap * k), 0.0)
                 dst[part, :] = tile
 
-        repeat(depth, one, 3)
+        repeat(depth, one, 6)
 
     far_rows = [(x, y, z) for x in (-1, 1) for z in (-1, 1) for y in (-1, 0, 1)]
     near_layers = [(0, y, z) for z in (-1, 1) for y in (-1, 0, 1)]
@@ -732,7 +732,7 @@
                 dy[at, :] = ahead - behind
 
     def spread(ref):
-        each_tile(lambda i: spread_tile(i, [ref[pl.ds(base_of(k, i), 8), :] for k in range(3)], set_a))
+        each_tile(lambda i: spread_tile(i, [ref[pl.ds(base_of(k, i), 8), :] for k in range(3)], set_a), 8)
 
     def couple(u_ref, sy_ref, dy_ref, i):
         def at(ref, k, dz):
@@ -795,7 +795,7 @@
                 set_a,
             )
 
-        each_tile(first)
+        each_tile(first, 8)
         bufs = [set_a, set_b]
         for sweep in range(SWEEPS - 1):
 

time: 77.2 us -> 76.2 us (0.987)
  Pallas kernels: 73.3 us -> 72.4 us
    pallas_call x1, Pallas kernels: 73.3 us -> 72.4 us  [body(): pl.pallas_call(functools.partial(kernel, sizes, cz), out_shape=(jax.Shape...]
where the time goes in v6:
time: 76.2 us; the launch traced here: 76.1 us
  Pallas kernels  72.4 us (95%)
  local copies, waits for them, and re-layouts  3.08 us (4%)
    pallas_call x1, Pallas kernels, body(): pl.pallas_call(functools.partial(kernel, sizes, cz), out_shape=(jax.Shape...  72.4 us
    unnamed x2, local copies, waits for them, and re-layouts  3.08 us

profile of v6, /device:TPU:1, one launch (start us, length us, event | category | flops | bytes accessed | tf_op | source)
XLA Modules:
  0.0 76.1 jit_solution(2823459450223141586)
XLA Ops:
  0.6 72.4 %schwarz_cg.1 = (f32[192,128]{1,0:T(8,128)}, f32[192,128]{1,0:T(8,128)}) custom-call(f32[192,128]{1,0:T(8,128)} %bitcast.4, s32[4,4,64]{2,1,0:T(4,128)} %labels_hbm.1, f32[8]{0:T(128)} %moduli.1, s32[64,128]{1,0:T(8,128)} %bitcast.7, f32[36,9216]{1,0:T(8,128)} %inverse.1, bf16[64,128]{1,0:T(8,128)(2,1)} %constant.10.clone.place_hbm, ...), custom_call_target="tpu_custom_call" | custom-call | tf_op jit(solution)/shard_map/schwarz_cg/pallas_call | solution.py:979
  73.0 1.5 %copy.14 = f32[3,8,8,128]{3,2,1,0:T(8,128)} copy(f32[3,8,8,128]{3,2,1,0:T(8,128)} %bitcast.6) | data formatting | bytes 196608
  74.5 1.5 %copy.15 = f32[3,8,8,128]{3,2,1,0:T(8,128)} copy(f32[3,8,8,128]{3,2,1,0:T(8,128)} %bitcast.5) | data formatting | bytes 196608
